TPU v7x, 32 devices: a whole 2x2x4 slice. The times are simulated.
32 devices in a mesh: replica: 2 (over x), shard: 16 (over z, y, core).
Axes of the slice: x: 2, y: 2, z: 4, core: 2. Of those that a mesh axis runs over, the one named last changes fastest.
Arguments:
- tokens: bfloat16 [32, 197, 768], P(('replica', 'shard')), may hold values from -6 to 6
- cotangent: bfloat16 [32, 197, 768], P(('replica', 'shard')), may hold values from -6 to 6
- norm1_gain: bfloat16 [768], P('shard'), may hold values from 0.5 to 1.5
- norm1_bias: bfloat16 [768], P('shard'), may hold values from -3 to 3
- proj_in: bfloat16 [768, 2304], P('shard'), may hold values from -0.21875 to 0.21875
- query_bias: bfloat16 [768], P('shard'), may hold values from -6 to 6
- value_bias: bfloat16 [768], P('shard'), may hold values from -3 to 3
- proj_out: bfloat16 [768, 768], P('shard'), may hold values from -0.625 to 0.625
- out_bias: bfloat16 [768], P('shard'), may hold values from -3 to 3
- norm2_gain: bfloat16 [768], P('shard'), may hold values from 0.5 to 1.5
- norm2_bias: bfloat16 [768], P('shard'), may hold values from -3 to 3
- router: bfloat16 [768, 16], P('shard'), may hold values from -0.21875 to 0.21875
- up_weight: bfloat16 [16, 768, 3072], P('shard'), may hold values from -0.21875 to 0.21875
- up_bias: bfloat16 [16, 3072], P('shard'), may hold values from -3 to 3
- down_weight: bfloat16 [16, 3072, 768], P('shard'), may hold values from -1.75 to 1.75
- down_bias: bfloat16 [16, 768], P('shard'), may hold values from -24 to 24
- expert_ids: int32 [6304, 2], P(('replica', 'shard')), may hold values from 0 to 15, as said below
- slot_ids: int32 [6304, 2], P(('replica', 'shard')), may hold values from 0 to 24, as said below
Outputs:
- block_out: bfloat16 [32, 197, 768], P(('replica', 'shard'))
- tokens_grad: bfloat16 [32, 197, 768], P(('replica', 'shard'))
- norm1_gain_grad: float32 [768], P('shard')
- norm1_bias_grad: float32 [768], P('shard')
- proj_in_grad: float32 [768, 2304], P('shard')
- query_bias_grad: float32 [768], P('shard')
- value_bias_grad: float32 [768], P('shard')
- proj_out_grad: float32 [768, 768], P('shard')
- out_bias_grad: float32 [768], P('shard')
- norm2_gain_grad: float32 [768], P('shard')
- norm2_bias_grad: float32 [768], P('shard')
- router_grad: float32 [768, 16], P('shard')
- up_weight_grad: float32 [16, 768, 3072], P('shard', None, 'replica')
- up_bias_grad: float32 [16, 3072], P('shard', 'replica')
- down_weight_grad: float32 [16, 3072, 768], P('shard', 'replica')
- down_bias_grad: float32 [16, 768], P('shard', 'replica')
Inputs may be any that keep to these rules, and one draw needn't show every extreme that they name: `expert_ids`: each row names two different experts. On every device the first 25 rows all name one expert first, the same expert on every device. `slot_ids`: within the rows of one device, first choices are placed before second choices, each in row order; a pair's slot is the number of that device's earlier pairs naming the same expert, stored as 24 when it is 24 or more, which marks a dropped pair. Kept pairs of one device never share an expert and a slot; on every device one expert has all 24 slots filled and a pair dropped.
All inputs are finite; a program needn't handle non-finite values.
Results may differ from a plain program's by a relative error of at most 0.022.
Values may be sent and summed in bfloat16 or wider, within the bound.
A program may use at most 128 MiB of HBM per device.

v0:
```python
import jax
import jax.numpy as jnp
from jax import lax
from jax.sharding import PartitionSpec as P

D = 768
HEADS = 12
HDIM = 64
SEQ = 197


EPS = 1e-06
SQRT_HALF = 0.7071067811865476
INV_ROOT_TWO_PI = 0.3989422804014327


def layer_norm(rows_in, norm_gain, norm_shift):
    average = jnp.mean(rows_in, axis=-1, keepdims=True)
    centred = rows_in - average
    inv_std = lax.rsqrt(jnp.mean(centred * centred, axis=-1, keepdims=True) + EPS)
    normed = centred * inv_std
    return (normed, inv_std, normed * norm_gain + norm_shift)


def norm_back(grad_rows, normed, inv_std, norm_gain):
    scaled = grad_rows * norm_gain
    inner = (
        scaled
        - jnp.mean(scaled, axis=-1, keepdims=True)
        - normed * jnp.mean(scaled * normed, axis=-1, keepdims=True)
    )
    return (inner * inv_std, jnp.sum(grad_rows * normed, axis=0), jnp.sum(grad_rows, axis=0))


def gelu_parts(pre_act):
    cumul = 0.5 * (1.0 + lax.erf(pre_act * SQRT_HALF))
    return (pre_act * cumul, cumul + pre_act * jnp.exp(-0.5 * pre_act * pre_act) * INV_ROOT_TWO_PI)


def route_table(expert_ids, slot_ids, experts, capacity):
    positions = jnp.arange(experts * capacity, dtype=jnp.int32)
    tables = []
    for choose in range(2):
        kept = slot_ids[:, choose] < capacity
        target = jnp.where(kept, expert_ids[:, choose] * capacity + slot_ids[:, choose], -1)
        tables.append((target[:, None] == positions[None, :]).astype(jnp.bfloat16))
    return tables


def pick_table(expert_ids, experts):
    labels = jnp.arange(experts, dtype=jnp.int32)
    return [
        (expert_ids[:, choose][:, None] == labels[None, :]).astype(jnp.float32)
        for choose in range(2)
    ]


def body(
    tokens,
    cotangent,
    norm1_gain,
    norm1_bias,
    proj_in,
    query_bias,
    value_bias,
    proj_out,
    out_bias,
    norm2_gain,
    norm2_bias,
    router,
    up_weight,
    up_bias,
    down_weight,
    down_bias,
    expert_ids,
    slot_ids,
):
    images = tokens.shape[0]
    gathered = (
        lax.all_gather(norm1_gain, "shard", axis=0, tiled=True),
        lax.all_gather(norm1_bias, "shard", axis=0, tiled=True),
        lax.all_gather(proj_in, "shard", axis=0, tiled=True),
        lax.all_gather(query_bias, "shard", axis=0, tiled=True),
        lax.all_gather(value_bias, "shard", axis=0, tiled=True),
        lax.all_gather(proj_out, "shard", axis=0, tiled=True),
        lax.all_gather(out_bias, "shard", axis=0, tiled=True),
        lax.all_gather(norm2_gain, "shard", axis=0, tiled=True),
        lax.all_gather(norm2_bias, "shard", axis=0, tiled=True),
        lax.all_gather(router, "shard", axis=0, tiled=True),
    )
    (
        gain_one,
        shift_one,
        proj_full,
        query_shift,
        value_shift,
        outproj_full,
        out_shift,
        gain_two,
        shift_two,
        router_full,
    ) = gathered
    tok_rows = tokens.reshape(-1, D).astype(jnp.float32)
    normed_one, inv_one, pre_one = layer_norm(
        tok_rows, gain_one.astype(jnp.float32), shift_one.astype(jnp.float32)
    )
    act_one = pre_one.astype(jnp.bfloat16)
    mixed = jnp.dot(act_one, proj_full, preferred_element_type=jnp.float32)
    query_part = (mixed[:, :D] + query_shift.astype(jnp.float32)).astype(jnp.bfloat16)
    key_part = mixed[:, D : 2 * D].astype(jnp.bfloat16)
    value_part = (mixed[:, 2 * D :] + value_shift.astype(jnp.float32)).astype(jnp.bfloat16)
    query_heads = query_part.reshape(images, SEQ, HEADS, HDIM)
    key_heads = key_part.reshape(images, SEQ, HEADS, HDIM)
    value_heads = value_part.reshape(images, SEQ, HEADS, HDIM)
    scores = jnp.einsum(
        "ishd,ithd->ihst", query_heads, key_heads, preferred_element_type=jnp.float32
    ) * HDIM ** (-0.5)
    log_total = jnp.log(jnp.sum(jnp.exp(scores), axis=-1))
    attn_probs = jnp.exp(scores - log_total[..., None]).astype(jnp.bfloat16)
    context = (
        jnp.einsum("ihst,ithd->ishd", attn_probs, value_heads, preferred_element_type=jnp.float32)
        .reshape(-1, D)
        .astype(jnp.bfloat16)
    )
    resid = (
        tok_rows
        + jnp.dot(context, outproj_full, preferred_element_type=jnp.float32)
        + out_shift.astype(jnp.float32)
    )
    normed_two, inv_two, pre_two = layer_norm(
        resid, gain_two.astype(jnp.float32), shift_two.astype(jnp.float32)
    )
    hidden = pre_two.astype(jnp.bfloat16)
    logits = jnp.dot(hidden, router_full, preferred_element_type=jnp.float32)
    exp_logits = jnp.exp(logits)
    gate_probs = exp_logits / jnp.sum(exp_logits, axis=-1, keepdims=True)
    local_experts = up_weight.shape[0]
    experts = local_experts * lax.axis_size("shard")
    capacity = 2 * tok_rows.shape[0] // experts
    routes = route_table(expert_ids, slot_ids, experts, capacity)
    picks = pick_table(expert_ids, experts)
    buffer = (
        (
            jnp.dot(routes[0].T, hidden, preferred_element_type=jnp.float32)
            + jnp.dot(routes[1].T, hidden, preferred_element_type=jnp.float32)
        )
        .astype(jnp.bfloat16)
        .reshape(experts, capacity, D)
    )
    arrived = lax.all_to_all(buffer, "shard", split_axis=0, concat_axis=1, tiled=True)
    expert_pre = (
        jnp.einsum("ecd,edf->ecf", arrived, up_weight, preferred_element_type=jnp.float32)
        + up_bias.astype(jnp.float32)[:, None, :]
    )
    act_val, slope = gelu_parts(expert_pre)
    active = act_val.astype(jnp.bfloat16)
    expert_out = (
        jnp.einsum("ecf,efd->ecd", active, down_weight, preferred_element_type=jnp.float32)
        + down_bias.astype(jnp.float32)[:, None, :]
    ).astype(jnp.bfloat16)
    returned = lax.all_to_all(expert_out, "shard", split_axis=1, concat_axis=0, tiled=True).reshape(
        experts * capacity, D
    )
    gathered_pair = [
        jnp.dot(table, returned, preferred_element_type=jnp.float32) for table in routes
    ]
    gate_pair = [jnp.sum(gate_probs * pick, axis=-1) for pick in picks]
    moe_sum = gate_pair[0][:, None] * gathered_pair[0] + gate_pair[1][:, None] * gathered_pair[1]
    block_out = (resid + moe_sum).astype(jnp.bfloat16).reshape(tokens.shape)
    grad_out = cotangent.reshape(-1, D).astype(jnp.float32)
    grad_gate = [jnp.sum(grad_out * part, axis=-1) for part in gathered_pair]
    sent = [(gate[:, None] * grad_out).astype(jnp.bfloat16) for gate in gate_pair]
    grad_buffer = (
        (
            jnp.dot(routes[0].T, sent[0], preferred_element_type=jnp.float32)
            + jnp.dot(routes[1].T, sent[1], preferred_element_type=jnp.float32)
        )
        .astype(jnp.bfloat16)
        .reshape(experts, capacity, D)
    )
    grad_arrived = lax.all_to_all(grad_buffer, "shard", split_axis=0, concat_axis=1, tiled=True)
    grad_active = jnp.einsum(
        "ecd,efd->ecf", grad_arrived, down_weight, preferred_element_type=jnp.float32
    )
    grad_pre = (grad_active * slope).astype(jnp.bfloat16)
    up_term = jnp.einsum("ecd,ecf->edf", arrived, grad_pre, preferred_element_type=jnp.float32)
    up_shift_term = jnp.sum(grad_pre, axis=1, dtype=jnp.float32)
    down_term = jnp.einsum("ecf,ecd->efd", active, grad_arrived, preferred_element_type=jnp.float32)
    down_shift_term = jnp.sum(grad_arrived, axis=1, dtype=jnp.float32)
    grad_in = jnp.einsum(
        "ecf,edf->ecd", grad_pre, up_weight, preferred_element_type=jnp.float32
    ).astype(jnp.bfloat16)
    grad_back = lax.all_to_all(grad_in, "shard", split_axis=1, concat_axis=0, tiled=True).reshape(
        experts * capacity, D
    )
    expert_grads = (
        lax.psum_scatter(
            up_term.astype(jnp.bfloat16), "replica", scatter_dimension=2, tiled=True
        ).astype(jnp.float32),
        lax.psum_scatter(
            up_shift_term.astype(jnp.bfloat16), "replica", scatter_dimension=1, tiled=True
        ).astype(jnp.float32),
        lax.psum_scatter(
            down_term.astype(jnp.bfloat16), "replica", scatter_dimension=1, tiled=True
        ).astype(jnp.float32),
        lax.psum_scatter(
            down_shift_term.astype(jnp.bfloat16), "replica", scatter_dimension=1, tiled=True
        ).astype(jnp.float32),
    )
    back_gain_one, back_proj, back_outproj, back_gain_two, back_router = (
        lax.all_gather(norm1_gain, "shard", axis=0, tiled=True),
        lax.all_gather(proj_in, "shard", axis=0, tiled=True),
        lax.all_gather(proj_out, "shard", axis=0, tiled=True),
        lax.all_gather(norm2_gain, "shard", axis=0, tiled=True),
        lax.all_gather(router, "shard", axis=0, tiled=True),
    )
    grad_moe = jnp.dot(routes[0], grad_back, preferred_element_type=jnp.float32) + jnp.dot(
        routes[1], grad_back, preferred_element_type=jnp.float32
    )
    grad_gates = picks[0] * grad_gate[0][:, None] + picks[1] * grad_gate[1][:, None]
    grad_logits = (
        gate_probs * (grad_gates - jnp.sum(gate_probs * grad_gates, axis=-1, keepdims=True))
    ).astype(jnp.bfloat16)
    router_term = jnp.dot(hidden.T, grad_logits, preferred_element_type=jnp.float32)
    grad_norm_two = grad_moe + jnp.dot(
        grad_logits, back_router.T, preferred_element_type=jnp.float32
    )
    grad_resid_two, gain_two_term, shift_two_term = norm_back(
        grad_norm_two, normed_two, inv_two, back_gain_two.astype(jnp.float32)
    )
    grad_resid = grad_out + grad_resid_two
    resid_bf = grad_resid.astype(jnp.bfloat16)
    out_shift_term = jnp.sum(grad_resid, axis=0)
    outproj_term = jnp.dot(context.T, resid_bf, preferred_element_type=jnp.float32)
    grad_context = (
        jnp.dot(resid_bf, back_outproj.T, preferred_element_type=jnp.float32)
        .astype(jnp.bfloat16)
        .reshape(images, SEQ, HEADS, HDIM)
    )
    scores_again = jnp.einsum(
        "ishd,ithd->ihst", query_heads, key_heads, preferred_element_type=jnp.float32
    ) * HDIM ** (-0.5)
    probs_full = jnp.exp(scores_again - log_total[..., None])
    grad_probs = jnp.einsum(
        "ishd,ithd->ihst", grad_context, value_heads, preferred_element_type=jnp.float32
    )
    grad_scores = (
        probs_full
        * (grad_probs - jnp.sum(probs_full * grad_probs, axis=-1, keepdims=True))
        * HDIM ** (-0.5)
    ).astype(jnp.bfloat16)
    probs_bf = probs_full.astype(jnp.bfloat16)
    grad_value = jnp.einsum(
        "ihst,ishd->ithd", probs_bf, grad_context, preferred_element_type=jnp.float32
    ).reshape(-1, D)
    grad_query = jnp.einsum(
        "ihst,ithd->ishd", grad_scores, key_heads, preferred_element_type=jnp.float32
    ).reshape(-1, D)
    grad_key = jnp.einsum(
        "ihst,ishd->ithd", grad_scores, query_heads, preferred_element_type=jnp.float32
    ).reshape(-1, D)
    grad_mixed = jnp.concatenate([grad_query, grad_key, grad_value], axis=1).astype(jnp.bfloat16)
    proj_term = jnp.dot(act_one.T, grad_mixed, preferred_element_type=jnp.float32)
    grad_act = jnp.dot(grad_mixed, back_proj.T, preferred_element_type=jnp.float32)
    grad_tok_norm, gain_one_term, shift_one_term = norm_back(
        grad_act, normed_one, inv_one, back_gain_one.astype(jnp.float32)
    )
    tokens_grad = (grad_resid + grad_tok_norm).astype(jnp.bfloat16).reshape(tokens.shape)
    query_shift_term = jnp.sum(grad_query, axis=0)
    value_shift_term = jnp.sum(grad_value, axis=0)
    shard_sums = (
        lax.psum_scatter(
            gain_one_term.astype(jnp.bfloat16), "shard", scatter_dimension=0, tiled=True
        ).astype(jnp.float32),
        lax.psum_scatter(
            shift_one_term.astype(jnp.bfloat16), "shard", scatter_dimension=0, tiled=True
        ).astype(jnp.float32),
        lax.psum_scatter(
            proj_term.astype(jnp.bfloat16), "shard", scatter_dimension=0, tiled=True
        ).astype(jnp.float32),
        lax.psum_scatter(
            query_shift_term.astype(jnp.bfloat16), "shard", scatter_dimension=0, tiled=True
        ).astype(jnp.float32),
        lax.psum_scatter(
            value_shift_term.astype(jnp.bfloat16), "shard", scatter_dimension=0, tiled=True
        ).astype(jnp.float32),
        lax.psum_scatter(
            outproj_term.astype(jnp.bfloat16), "shard", scatter_dimension=0, tiled=True
        ).astype(jnp.float32),
        lax.psum_scatter(
            out_shift_term.astype(jnp.bfloat16), "shard", scatter_dimension=0, tiled=True
        ).astype(jnp.float32),
        lax.psum_scatter(
            gain_two_term.astype(jnp.bfloat16), "shard", scatter_dimension=0, tiled=True
        ).astype(jnp.float32),
        lax.psum_scatter(
            shift_two_term.astype(jnp.bfloat16), "shard", scatter_dimension=0, tiled=True
        ).astype(jnp.float32),
        lax.psum_scatter(
            router_term.astype(jnp.bfloat16), "shard", scatter_dimension=0, tiled=True
        ).astype(jnp.float32),
    )
    dense_grads = (
        lax.psum(shard_sums[0].astype(jnp.bfloat16), "replica").astype(jnp.float32),
        lax.psum(shard_sums[1].astype(jnp.bfloat16), "replica").astype(jnp.float32),
        lax.psum(shard_sums[2].astype(jnp.bfloat16), "replica").astype(jnp.float32),
        lax.psum(shard_sums[3].astype(jnp.bfloat16), "replica").astype(jnp.float32),
        lax.psum(shard_sums[4].astype(jnp.bfloat16), "replica").astype(jnp.float32),
        lax.psum(shard_sums[5].astype(jnp.bfloat16), "replica").astype(jnp.float32),
        lax.psum(shard_sums[6].astype(jnp.bfloat16), "replica").astype(jnp.float32),
        lax.psum(shard_sums[7].astype(jnp.bfloat16), "replica").astype(jnp.float32),
        lax.psum(shard_sums[8].astype(jnp.bfloat16), "replica").astype(jnp.float32),
        lax.psum(shard_sums[9].astype(jnp.bfloat16), "replica").astype(jnp.float32),
    )
    return (
        block_out,
        tokens_grad,
        dense_grads[0],
        dense_grads[1],
        dense_grads[2],
        dense_grads[3],
        dense_grads[4],
        dense_grads[5],
        dense_grads[6],
        dense_grads[7],
        dense_grads[8],
        dense_grads[9],
        expert_grads[0],
        expert_grads[1],
        expert_grads[2],
        expert_grads[3],
    )


def solution(mesh):
    in_specs = (
        P(("replica", "shard"), None, None),
        P(("replica", "shard"), None, None),
        P("shard"),
        P("shard"),
        P("shard", None),
        P("shard"),
        P("shard"),
        P("shard", None),
        P("shard"),
        P("shard"),
        P("shard"),
        P("shard", None),
        P("shard", None, None),
        P("shard", None),
        P("shard", None, None),
        P("shard", None),
        P(("replica", "shard"), None),
        P(("replica", "shard"), None),
    )
    out_specs = (
        P(("replica", "shard"), None, None),
        P(("replica", "shard"), None, None),
        P("shard"),
        P("shard"),
        P("shard", None),
        P("shard"),
        P("shard"),
        P("shard", None),
        P("shard"),
        P("shard"),
        P("shard"),
        P("shard", None),
        P("shard", None, "replica"),
        P("shard", "replica"),
        P("shard", "replica", None),
        P("shard", "replica"),
    )
    return jax.shard_map(body, mesh=mesh, in_specs=in_specs, out_specs=out_specs, check_vma=False)
```

profile of v0, /device:TPU:0, one launch (start us, length us, event | category | flops | bytes accessed | tf_op | source)
XLA Modules:
  0.0 628.0 jit_solution(12386694060292079146)
XLA Ops:
  16.5 63.8 %all-reduce.15 = (bf16[768]{0:T(1024)(128)(2,1)S(1)}, bf16[768]{0:T(1024)(128)(2,1)S(1)}, bf16[768]{0:T(1024)(128)(2,1)S(1)}, bf16[768]{0:T(1024)(128)(2,1)S(1)}...) all-reduce(bf16[768]{0:T(1024)(128)(2,1)S(1)} %dynamic-update-slice, ...), channel_id=1, replica_groups=mesh['replica'=2,'shard'=16] {'shard'}, use_global_device_ids=true, to_apply=%add.1 | all-reduce | flops 5376 | bytes 21504
  93.2 6.6 %all-gather.6.cloned.1.call-done = bf16[768,768]{1,0:T(8,128)(2,1)} async-done(((bf16[48,768]{1,0:T(8,128)(2,1)}), bf16[768,768]{1,0:T(8,128)(2,1)}) %all-gather.6.cloned.1.call-update) | async-done | bytes 1179664 | tf_op jit(solution)/shard_map/all_gather | solution.py:85
  108.2 15.3 %all-to-all-done = bf16[16,24,768]{2,1,0:T(8,128)(2,1)S(1)} async-done(((bf16[16,24,768]{2,1,0:T(8,128)(2,1)}), bf16[16,24,768]{2,1,0:T(8,128)(2,1)S(1)}, u32[]{:S(2)}, u32[]{:S(2)}) %all-to-all-start) | async-done | bytes 589856 | tf_op jit(solution)/shard_map/all_to_all | solution.py:150
  123.5 6.5 %multiply_convert_fusion = (bf16[384,3072]{1,0:T(8,128)(2,1)S(1)}, f32[384,3072]{1,0:T(8,128)}) fusion(f32[3072]{0:T(1024)S(1)} %bitcast.232, bf16[384,768]{1,0:T(8,128)(2,1)S(1)} %bitcast.214, bf16[1,768,3072]{2,1,0:T(8,128)(2,1)} %param.30), kind=kOutput, calls=%fused_computation.20 | convolution fusion | flops 1819017216 | bytes 12398592 | tf_op jit(solution)/shard_map/ecd,edf->ecf/dot_general | solution.py:152
  130.1 5.2 fusion.59
  142.0 4.6 all-to-all-start.1
  146.7 26.3 %all-gather = bf16[16,48,16]{1,2,0:T(8,128)(2,1)S(1)} all-gather(bf16[1,48,16]{1,2,0:T(8,128)(2,1)S(1)} %bitcast.233), channel_id=1, replica_groups=mesh['replica'=2,'shard'=16] {'shard'}, dimensions={0}, use_global_device_ids=true | all-gather | bytes 26112 | tf_op jit(solution)/shard_map/all_gather | solution.py:89
  179.7 20.7 %all_to_all.16 = bf16[16,24,768]{2,1,0:T(8,128)(2,1)S(1)} all-to-all(bf16[16,24,768]{2,1,0:T(8,128)(2,1)S(1)} %bitcast.199), channel_id=1, replica_groups=mesh['replica'=2,'shard'=16] {'shard'}, dimensions={0} | all-to-all | bytes 1179648 | tf_op jit(solution)/shard_map/all_to_all | solution.py:181
  200.4 6.5 %fusion.158 = (bf16[3072]{0:T(1024)(128)(2,1)}, bf16[384,3072]{1,0:T(8,128)(2,1)S(1)}) fusion(f32[384,3072]{1,0:T(8,128)} %get-tuple-element.71, bf16[384,768]{1,0:T(8,128)(2,1)S(1)} %bitcast.200, bf16[1,3072,768]{2,1,0:T(8,128)(2,1)} %param.32), kind=kOutput, calls=%fused_computation.175 | convolution fusion | flops 1824912384 | bytes 12392448 | tf_op jit(solution)/shard_map/ecd,efd->ecf/dot_general | solution.py:182
  210.9 5.2 reduce.16
  221.6 15.2 %all-to-all-done.3 = bf16[16,2,9216]{2,1,0:T(2,128)(2,1)} async-done(((bf16[16,2,9216]{2,1,0:T(2,128)(2,1)}), bf16[16,2,9216]{2,1,0:T(2,128)(2,1)}, u32[]{:S(2)}, u32[]{:S(2)}) %all-to-all-start.3) | async-done | bytes 589856 | tf_op jit(solution)/shard_map/all_to_all | solution.py:193
  256.2 4.8 fusion.56
  261.0 5.0 fusion.150
  273.4 31.5 %reduce-scatter.16.cloned.1.call-done = bf16[48,768]{1,0:T(8,128)(2,1)} async-done(((bf16[768,768]{1,0:T(8,128)(2,1)}), bf16[48,768]{1,0:T(8,128)(2,1)}) %reduce-scatter.16.cloned.1.call-update) | async-done | bytes 73744 | tf_op jit(solution)/shard_map/reduce_scatter | solution.py:287
  304.9 71.6 %reduce-scatter.14.cloned.1.call-done = bf16[48,2304]{1,0:T(8,128)(2,1)} async-done(((bf16[768,2304]{1,0:T(8,128)(2,1)}), bf16[48,2304]{1,0:T(8,128)(2,1)}) %reduce-scatter.14.cloned.1.call-update) | async-done | bytes 221200 | tf_op jit(solution)/shard_map/reduce_scatter | solution.py:278
  376.6 5.9 fusion.16
  382.9 6.4 %fusion.17 = bf16[1,3072,768]{2,1,0:T(8,128)(2,1)} fusion(bf16[384,3072]{1,0:T(8,128)(2,1)} %copy-done.41, bf16[384,768]{1,0:T(8,128)(2,1)S(1)} %bitcast.201), kind=kOutput, calls=%fused_computation.23 | convolution fusion | flops 1814298624 | bytes 7667712 | tf_op jit(solution)/shard_map/ecf,ecd->efd/dot_general | solution.py:188
  390.1 42.5 %reduce-scatter.22.cloned.1.call-done = bf16[48,16]{1,0:T(8,128)(2,1)} async-done(((bf16[768,16]{1,0:T(8,128)(2,1)}), bf16[48,16]{1,0:T(8,128)(2,1)}) %reduce-scatter.22.cloned.1.call-update) | async-done | bytes 1552
  433.3 11.4 %reduce-scatter.26.cloned.1.call-done = bf16[384,1]{1,0:T(8,128)(2,1)} async-done(((bf16[768,1]{1,0:T(8,128)(2,1)}), bf16[384,1]{1,0:T(8,128)(2,1)}) %reduce-scatter.26.cloned.1.call-update) | async-done | bytes 784
  446.3 18.8 %reduce-scatter.24.cloned.1.call-done = bf16[1536,1]{1,0:T(8,128)(2,1)} async-done(((bf16[3072,1]{1,0:T(8,128)(2,1)}), bf16[1536,1]{1,0:T(8,128)(2,1)}) %reduce-scatter.24.cloned.1.call-update) | async-done | bytes 3088
  470.6 61.0 %all-reduce.14 = (bf16[768]{0:T(1024)(128)(2,1)S(1)}, bf16[768]{0:T(1024)(128)(2,1)S(1)}, bf16[768]{0:T(1024)(128)(2,1)S(1)}, bf16[768]{0:T(1024)(128)(2,1)S(1)}...) all-reduce(bf16[768]{0:T(1024)(128)(2,1)S(1)} %get-tuple-element.18, ...), channel_id=2, replica_groups=mesh['replica'=2,'shard'=16] {'shard'}, use_global_device_ids=true, to_apply=%region_17.18.clone | all-reduce | flops 5376 | bytes 21504
  532.2 5.3 all-reduce.16
  546.0 8.5 %reduce-scatter.18.cloned.1.call-done = bf16[1,768,1536]{2,1,0:T(8,128)(2,1)} async-done(((bf16[1,768,3072]{2,1,0:T(8,128)(2,1)}), bf16[1,768,1536]{2,1,0:T(8,128)(2,1)}) %reduce-scatter.18.cloned.1.call-update) | async-done | bytes 2359312 | tf_op jit(solution)/shard_map/reduce_scatter | solution.py:197
  559.0 57.7 %reduce-scatter.20.cloned.1.call-done = bf16[1,1536,768]{2,1,0:T(8,128)(2,1)} async-done(((bf16[1,3072,768]{2,1,0:T(8,128)(2,1)}), bf16[1,1536,768]{2,1,0:T(8,128)(2,1)}) %reduce-scatter.20.cloned.1.call-update) | async-done | bytes 2359312 | tf_op jit(solution)/shard_map/reduce_scatter | solution.py:203
  (222 shorter events, 105.0 us)
Async XLA Ops:
  7.2 78.0 %all-gather.4.cloned.1.call-start = ((), (), s32[]{:S(2)}) async-start(), calls=%async_computation.11 | async-start | bytes 3760128 | tf_op jit(solution)/shard_map/all_gather | solution.py:82
  7.9 92.0 %all-gather.6.cloned.1.call-start = ((), (), s32[]{:S(2)}) async-start(), calls=%async_computation.12 | async-start | bytes 1253376 | tf_op jit(solution)/shard_map/all_gather | solution.py:85
  104.0 19.5 %all-to-all-start = ((bf16[16,24,768]{2,1,0:T(8,128)(2,1)}), bf16[16,24,768]{2,1,0:T(8,128)(2,1)S(1)}, u32[]{:S(2)}, u32[]{:S(2)}) async-start(bf16[16,24,768]{2,1,0:T(8,128)(2,1)} %bitcast.12), calls=%async_computation | async-start | bytes 1179648 | tf_op jit(solution)/shard_map/all_to_all | solution.py:150
  136.2 10.5 %copy-start.34 = (bf16[48,16]{0,1:T(8,128)(2,1)S(1)}, bf16[48,16]{0,1:T(8,128)(2,1)}, u32[]{:S(2)}) copy-start(bf16[48,16]{0,1:T(8,128)(2,1)} %param.29) | copy-start | bytes 4612
  142.0 34.8 %copy-start.1 = (bf16[1,197,768]{2,1,0:T(8,128)(2,1)S(1)}, bf16[1,197,768]{2,1,0:T(8,128)(2,1)}, u32[]{:S(2)}) copy-start(bf16[1,197,768]{2,1,0:T(8,128)(2,1)} %param.19) | copy-start | bytes 907780
  142.0 31.4 %all-to-all-start.1 = ((bf16[16,2,9216]{2,1,0:T(2,128)(2,1)}), bf16[16,2,9216]{2,1,0:T(2,128)(2,1)S(1)}, u32[]{:S(2)}, u32[]{:S(2)}) async-start(bf16[16,2,9216]{2,1,0:T(2,128)(2,1)} %reshape.343), calls=%async_computation.1 | async-start | bytes 1179648 | tf_op jit(solution)/shard_map/all_to_all | solution.py:161
  178.7 42.7 %copy-start.29 = (f32[197]{0:T(256)}, f32[197]{0:T(256)S(1)}, u32[]{:S(2)}) copy-start(f32[197]{0:T(256)S(1)} %get-tuple-element.26) | copy-start | bytes 2368
  179.7 27.2 %slice-start = ((s8[4718592]{0:T(1024)(128)(4,1)}), s8[4194304]{0:T(1024)(128)(4,1)S(1)}, s32[]{:S(2)}) async-start(s8[4718592]{0:T(1024)(128)(4,1)} %bitcast.234), calls=%async_computation.21 | async-start | bytes 8388608
  217.1 19.8 %all-to-all-start.3 = ((bf16[16,2,9216]{2,1,0:T(2,128)(2,1)}), bf16[16,2,9216]{2,1,0:T(2,128)(2,1)}, u32[]{:S(2)}, u32[]{:S(2)}) async-start(bf16[16,2,9216]{2,1,0:T(2,128)(2,1)} %reshape.345), calls=%async_computation.3 | async-start | bytes 1179648 | tf_op jit(solution)/shard_map/all_to_all | solution.py:193
  221.3 83.6 %reduce-scatter.16.cloned.1.call-start = ((), (), s32[]{:S(2)}) async-start(), calls=%async_computation.14 | async-start | bytes 1253376 | tf_op jit(solution)/shard_map/reduce_scatter | solution.py:287
  247.1 129.4 %reduce-scatter.14.cloned.1.call-start = ((), (), s32[]{:S(2)}) async-start(), calls=%async_computation.13 | async-start | bytes 3760128 | tf_op jit(solution)/shard_map/reduce_scatter | solution.py:278
  254.2 11.8 %copy-start.36 = (bf16[1,197,12,64]{1,3,2,0:T(8,128)(2,1)}, bf16[1,197,12,64]{1,3,2,0:T(8,128)(2,1)S(1)}, u32[]{:S(2)}) copy-start(bf16[1,197,12,64]{1,3,2,0:T(8,128)(2,1)S(1)} %get-tuple-element.58) | copy-start | bytes 907780
  256.2 9.9 %copy-start.19 = (f32[197]{0:T(256)S(1)}, f32[197]{0:T(256)}, u32[]{:S(2)}) copy-start(f32[197]{0:T(256)} %copy-done.18) | copy-start | bytes 2368
  256.2 9.9 %copy-start.21 = (f32[768]{0:T(1024)S(1)}, f32[768]{0:T(1024)}, u32[]{:S(2)}) copy-start(f32[768]{0:T(1024)} %copy-done.20) | copy-start | bytes 9220
  256.2 9.9 %copy-start.28 = (f32[197]{0:T(256)S(1)}, f32[197]{0:T(256)}, u32[]{:S(2)}) copy-start(f32[197]{0:T(256)} %copy-done.27) | copy-start | bytes 2368
  269.2 107.4 %copy-start.13 = (bf16[16,24,768]{2,1,0:T(8,128)(2,1)S(1)}, bf16[16,24,768]{2,1,0:T(8,128)(2,1)}, u32[]{:S(2)}) copy-start(bf16[16,24,768]{2,1,0:T(8,128)(2,1)} %copy-done.12) | copy-start | bytes 1769476
  269.2 163.3 %reduce-scatter.22.cloned.1.call-start = ((), (), s32[]{:S(2)}) async-start(), calls=%async_computation.17 | async-start | bytes 208896
  270.9 173.9 %reduce-scatter.26.cloned.1.call-start = ((), (), s32[]{:S(2)}) async-start(), calls=%async_computation.19 | async-start | bytes 294912
  271.9 193.2 %reduce-scatter.24.cloned.1.call-start = ((), (), s32[]{:S(2)}) async-start(), calls=%async_computation.18 | async-start | bytes 1179648
  273.4 269.3 %all-reduce.20.cloned.1.call-start = ((), (), s32[]{:S(2)}) async-start(), calls=%async_computation.20 | async-start | bytes 589824 | tf_op jit(solution)/shard_map/psum | solution.py:306
  376.5 177.9 %reduce-scatter.18.cloned.1.call-start = ((), (), s32[]{:S(2)}) async-start(), calls=%async_computation.15 | async-start | bytes 7077888 | tf_op jit(solution)/shard_map/reduce_scatter | solution.py:197
  382.6 234.2 %reduce-scatter.20.cloned.1.call-start = ((), (), s32[]{:S(2)}) async-start(), calls=%async_computation.16 | async-start | bytes 7077888 | tf_op jit(solution)/shard_map/reduce_scatter | solution.py:203
  389.3 77.8 %copy-start.37 = (bf16[1,197,12,64]{1,3,2,0:T(8,128)(2,1)S(1)}, bf16[1,197,12,64]{1,3,2,0:T(8,128)(2,1)}, u32[]{:S(2)}) copy-start(bf16[1,197,12,64]{1,3,2,0:T(8,128)(2,1)} %copy-done.36) | copy-start | bytes 907780
  389.3 77.8 %copy-start.39 = (bf16[12,64,197]{2,1,0:T(8,128)(2,1)S(1)}, bf16[12,64,197]{2,1,0:T(8,128)(2,1)}, u32[]{:S(2)}) copy-start(bf16[12,64,197]{2,1,0:T(8,128)(2,1)} %copy-done.38) | copy-start | bytes 907780
  (33 other events, 145.6 us)
Sparse Core Ops, SparseCore 0:
  10.3 50.2 all-gather.3
  62.9 36.9 all-gather.5
  247.2 57.6 reduce-scatter.15
  309.2 67.2 reduce-scatter.13
  380.4 52.1 reduce-scatter.21
  434.6 10.0 reduce-scatter.25
  447.6 17.5 reduce-scatter.23
  467.5 23.7 all-reduce.19
  494.2 60.2 reduce-scatter.17
  556.6 60.0 reduce-scatter.19
where the time goes:
time: 635 us; the launch traced here: 628 us
  waiting for transfers between devices  281 us (44%)
  blocking collectives  177 us (28%)
  matrix products  78.5 us (12%)
  other arithmetic  34.6 us (5%)
  local copies, waits for them, and re-layouts  26.8 us (4%)
  between operations  16.5 us (3%)
  starting transfers between devices  13.8 us (2%)
    unnamed x2, blocking collectives  125 us
    unnamed x13, waiting for transfers between devices  74.2 us
    reduce_scatter x1, waiting for transfers between devices, body(): lax.psum_scatter(proj_term.astype(jnp.bfloat16), 'shard', scatter_dimensi...  71.6 us
    reduce_scatter x1, waiting for transfers between devices, body(): lax.psum_scatter(down_term.astype(jnp.bfloat16), 'replica', scatter_dimen...  57.7 us
    reduce_scatter x1, waiting for transfers between devices, body(): lax.psum_scatter(outproj_term.astype(jnp.bfloat16), 'shard', scatter_dime...  31.5 us
    all_gather x1, blocking collectives, body(): lax.all_gather(router, 'shard', axis=0, tiled=True)  26.3 us
    unnamed x122, local copies, waits for them, and re-layouts  22.3 us
    all_to_all x1, blocking collectives, body(): lax.all_to_all(grad_buffer, 'shard', split_axis=0, concat_axis=1, tiled=T...  20.7 us
  transfers between devices with their start and end apart: 13, of which 10 were waited for; matrix products, arithmetic and copies ran while one was open for 13% of the time, Pallas kernels for 0%

commit v1 on v0

v1 whole, which is shorter than its diff:
```python
import jax
import jax.numpy as jnp
from jax import lax
from jax.sharding import PartitionSpec as P

D = 768
HEADS = 12
HDIM = 64
SEQ = 197


EPS = 1e-06
SQRT_HALF = 0.7071067811865476
INV_ROOT_TWO_PI = 0.3989422804014327


def layer_norm(rows_in, norm_gain, norm_shift):
    average = jnp.mean(rows_in, axis=-1, keepdims=True)
    centred = rows_in - average
    inv_std = lax.rsqrt(jnp.mean(centred * centred, axis=-1, keepdims=True) + EPS)
    normed = centred * inv_std
    return (normed, inv_std, normed * norm_gain + norm_shift)


def norm_back(grad_rows, normed, inv_std, norm_gain):
    scaled = grad_rows * norm_gain
    inner = (
        scaled
        - jnp.mean(scaled, axis=-1, keepdims=True)
        - normed * jnp.mean(scaled * normed, axis=-1, keepdims=True)
    )
    return (inner * inv_std, jnp.sum(grad_rows * normed, axis=0), jnp.sum(grad_rows, axis=0))


def gelu_parts(pre_act):
    cumul = 0.5 * (1.0 + lax.erf(pre_act * SQRT_HALF))
    return (pre_act * cumul, cumul + pre_act * jnp.exp(-0.5 * pre_act * pre_act) * INV_ROOT_TWO_PI)


def route_table(expert_ids, slot_ids, experts, capacity):
    positions = jnp.arange(experts * capacity, dtype=jnp.int32)
    tables = []
    for choose in range(2):
        kept = slot_ids[:, choose] < capacity
        target = jnp.where(kept, expert_ids[:, choose] * capacity + slot_ids[:, choose], -1)
        tables.append((target[:, None] == positions[None, :]).astype(jnp.bfloat16))
    return tables


def pick_table(expert_ids, experts):
    labels = jnp.arange(experts, dtype=jnp.int32)
    return [
        (expert_ids[:, choose][:, None] == labels[None, :]).astype(jnp.float32)
        for choose in range(2)
    ]


def lane_pad(blocks):
    rows = blocks[0].shape[0]
    spare = -sum(block.shape[1] for block in blocks) % 128
    return jnp.concatenate(blocks + [jnp.zeros((rows, spare), blocks[0].dtype)], axis=1)


def other_replicas(value):
    size = lax.axis_size("replica")
    return [
        lax.ppermute(value, "replica", [(at, (at + step) % size) for at in range(size)])
        for step in range(1, size)
    ]


def to_expert(value, local_experts, capacity):
    shards, width = value.shape[0], value.shape[-1]
    return (
        value.reshape(shards, local_experts, capacity, width)
        .swapaxes(0, 1)
        .reshape(local_experts, shards * capacity, width)
    )


def from_expert(value, shards, capacity):
    local_experts, width = value.shape[0], value.shape[-1]
    return (
        value.reshape(local_experts, shards, capacity, width)
        .swapaxes(0, 1)
        .reshape(shards, local_experts * capacity, width)
    )


def expert_middle(rows, grad_rows, up_weight, up_bias, down_weight):
    expert_pre = (
        jnp.einsum("ecd,edf->ecf", rows, up_weight, preferred_element_type=jnp.float32)
        + up_bias.astype(jnp.float32)[:, None, :]
    )
    act_val, slope = gelu_parts(expert_pre)
    grad_active = jnp.einsum(
        "ecd,efd->ecf", grad_rows, down_weight, preferred_element_type=jnp.float32
    )
    return (act_val.astype(jnp.bfloat16), (grad_active * slope).astype(jnp.bfloat16))


def body(
    tokens,
    cotangent,
    norm1_gain,
    norm1_bias,
    proj_in,
    query_bias,
    value_bias,
    proj_out,
    out_bias,
    norm2_gain,
    norm2_bias,
    router,
    up_weight,
    up_bias,
    down_weight,
    down_bias,
    expert_ids,
    slot_ids,
):
    images = tokens.shape[0]
    small = jnp.stack(
        [norm1_gain, norm1_bias, query_bias, value_bias, out_bias, norm2_gain, norm2_bias],
        axis=1,
    )
    width_in, width_small = proj_in.shape[1], small.shape[1] + router.shape[1]
    first = lax.all_gather(
        lane_pad([proj_in, small, router]), "shard", axis=0, tiled=True
    )
    outproj_full = lax.all_gather(proj_out, "shard", axis=0, tiled=True)
    proj_full = first[:, :width_in]
    small_full = first[:, width_in : width_in + small.shape[1]]
    router_full = first[:, width_in + small.shape[1] : width_in + width_small]
    (
        gain_one,
        shift_one,
        query_shift,
        value_shift,
        out_shift,
        gain_two,
        shift_two,
    ) = [row for row in small_full.T]
    tok_rows = tokens.reshape(-1, D).astype(jnp.float32)
    normed_one, inv_one, pre_one = layer_norm(
        tok_rows, gain_one.astype(jnp.float32), shift_one.astype(jnp.float32)
    )
    act_one = pre_one.astype(jnp.bfloat16)
    mixed = jnp.dot(act_one, proj_full, preferred_element_type=jnp.float32)
    query_part = (mixed[:, :D] + query_shift.astype(jnp.float32)).astype(jnp.bfloat16)
    key_part = mixed[:, D : 2 * D].astype(jnp.bfloat16)
    value_part = (mixed[:, 2 * D :] + value_shift.astype(jnp.float32)).astype(jnp.bfloat16)
    query_heads = query_part.reshape(images, SEQ, HEADS, HDIM)
    key_heads = key_part.reshape(images, SEQ, HEADS, HDIM)
    value_heads = value_part.reshape(images, SEQ, HEADS, HDIM)
    scores = jnp.einsum(
        "ishd,ithd->ihst", query_heads, key_heads, preferred_element_type=jnp.float32
    ) * HDIM ** (-0.5)
    log_total = jnp.log(jnp.sum(jnp.exp(scores), axis=-1))
    attn_probs = jnp.exp(scores - log_total[..., None]).astype(jnp.bfloat16)
    context = (
        jnp.einsum("ihst,ithd->ishd", attn_probs, value_heads, preferred_element_type=jnp.float32)
        .reshape(-1, D)
        .astype(jnp.bfloat16)
    )
    resid = (
        tok_rows
        + jnp.dot(context, outproj_full, preferred_element_type=jnp.float32)
        + out_shift.astype(jnp.float32)
    )
    normed_two, inv_two, pre_two = layer_norm(
        resid, gain_two.astype(jnp.float32), shift_two.astype(jnp.float32)
    )
    hidden = pre_two.astype(jnp.bfloat16)
    logits = jnp.dot(hidden, router_full, preferred_element_type=jnp.float32)
    exp_logits = jnp.exp(logits)
    gate_probs = exp_logits / jnp.sum(exp_logits, axis=-1, keepdims=True)
    local_experts = up_weight.shape[0]
    experts = local_experts * lax.axis_size("shard")
    capacity = 2 * tok_rows.shape[0] // experts
    routes = route_table(expert_ids, slot_ids, experts, capacity)
    picks = pick_table(expert_ids, experts)
    both = jnp.concatenate(routes, axis=0)
    either = routes[0] + routes[1]
    gate_pair = [jnp.sum(gate_probs * pick, axis=-1) for pick in picks]
    grad_out = cotangent.reshape(-1, D).astype(jnp.float32)
    sent = jnp.concatenate(
        [(gate[:, None] * grad_out).astype(jnp.bfloat16) for gate in gate_pair], axis=0
    )
    buffer = jnp.dot(either.T, hidden, preferred_element_type=jnp.float32)
    grad_buffer = jnp.dot(both.T, sent, preferred_element_type=jnp.float32)
    shards = lax.axis_size("shard")
    outgoing = (
        jnp.concatenate([buffer, grad_buffer], axis=1)
        .astype(jnp.bfloat16)
        .reshape(shards, local_experts * capacity, 2 * D)
    )
    landed = to_expert(
        lax.all_to_all(outgoing, "shard", split_axis=0, concat_axis=0, tiled=True),
        local_experts,
        capacity,
    )
    arrived, grad_arrived = landed[..., :D], landed[..., D:]
    others = other_replicas(landed)
    active, grad_pre = expert_middle(arrived, grad_arrived, up_weight, up_bias, down_weight)
    expert_out = (
        jnp.einsum("ecf,efd->ecd", active, down_weight, preferred_element_type=jnp.float32)
        + down_bias.astype(jnp.float32)[:, None, :]
    ).astype(jnp.bfloat16)
    grad_in = jnp.einsum(
        "ecf,edf->ecd", grad_pre, up_weight, preferred_element_type=jnp.float32
    ).astype(jnp.bfloat16)
    answer = from_expert(jnp.concatenate([expert_out, grad_in], axis=2), shards, capacity)
    back = lax.all_to_all(answer, "shard", split_axis=0, concat_axis=0, tiled=True).reshape(
        experts * capacity, 2 * D
    )
    returned, grad_back = back[:, :D], back[:, D:]

    replicas = lax.axis_size("replica")
    ours = lax.axis_index("replica")
    part = up_weight.shape[2] // replicas
    up_part = lax.dynamic_slice_in_dim(up_weight, ours * part, part, axis=2)
    up_bias_part = lax.dynamic_slice_in_dim(up_bias, ours * part, part, axis=1)
    down_part = lax.dynamic_slice_in_dim(down_weight, ours * part, part, axis=1)
    active_parts = [lax.dynamic_slice_in_dim(active, ours * part, part, axis=2)]
    grad_pre_parts = [lax.dynamic_slice_in_dim(grad_pre, ours * part, part, axis=2)]
    for other in others:
        other_active, other_pre = expert_middle(
            other[..., :D], other[..., D:], up_part, up_bias_part, down_part
        )
        active_parts.append(other_active)
        grad_pre_parts.append(other_pre)
    all_rows = jnp.concatenate([landed] + others, axis=1)
    all_active = jnp.concatenate(active_parts, axis=1)
    all_pre = jnp.concatenate(grad_pre_parts, axis=1)
    width_part = D // replicas
    expert_grads = (
        jnp.einsum("ecd,ecf->edf", all_rows[..., :D], all_pre, preferred_element_type=jnp.float32),
        jnp.sum(all_pre, axis=1, dtype=jnp.float32),
        jnp.einsum(
            "ecf,ecd->efd", all_active, all_rows[..., D:], preferred_element_type=jnp.float32
        ),
        lax.dynamic_slice_in_dim(
            jnp.sum(all_rows[..., D:], axis=1, dtype=jnp.float32),
            ours * width_part,
            width_part,
            axis=1,
        ),
    )

    rows_here = tok_rows.shape[0]
    gathered_both = jnp.dot(both, returned, preferred_element_type=jnp.float32)
    gathered_pair = [gathered_both[:rows_here], gathered_both[rows_here:]]
    moe_sum = gate_pair[0][:, None] * gathered_pair[0] + gate_pair[1][:, None] * gathered_pair[1]
    block_out = (resid + moe_sum).astype(jnp.bfloat16).reshape(tokens.shape)
    grad_gate = [jnp.sum(grad_out * part_k, axis=-1) for part_k in gathered_pair]
    back_gain_one, back_proj, back_outproj, back_gain_two, back_router = (
        gain_one,
        proj_full,
        outproj_full,
        gain_two,
        router_full,
    )
    grad_moe = jnp.dot(either, grad_back, preferred_element_type=jnp.float32)
    grad_gates = picks[0] * grad_gate[0][:, None] + picks[1] * grad_gate[1][:, None]
    grad_logits = (
        gate_probs * (grad_gates - jnp.sum(gate_probs * grad_gates, axis=-1, keepdims=True))
    ).astype(jnp.bfloat16)
    router_term = jnp.dot(hidden.T, grad_logits, preferred_element_type=jnp.float32)
    grad_norm_two = grad_moe + jnp.dot(
        grad_logits, back_router.T, preferred_element_type=jnp.float32
    )
    grad_resid_two, gain_two_term, shift_two_term = norm_back(
        grad_norm_two, normed_two, inv_two, back_gain_two.astype(jnp.float32)
    )
    grad_resid = grad_out + grad_resid_two
    resid_bf = grad_resid.astype(jnp.bfloat16)
    out_shift_term = jnp.sum(grad_resid, axis=0)
    outproj_term = jnp.dot(context.T, resid_bf, preferred_element_type=jnp.float32)
    early = lax.psum_scatter(
        lane_pad(
            [
                outproj_term.astype(jnp.bfloat16),
                jnp.stack([out_shift_term, gain_two_term, shift_two_term], axis=0)
                .astype(jnp.bfloat16)
                .T,
                router_term.astype(jnp.bfloat16),
            ]
        ),
        "shard",
        scatter_dimension=0,
        tiled=True,
    )
    grad_context = (
        jnp.dot(resid_bf, back_outproj.T, preferred_element_type=jnp.float32)
        .astype(jnp.bfloat16)
        .reshape(images, SEQ, HEADS, HDIM)
    )
    scores_again = jnp.einsum(
        "ishd,ithd->ihst", query_heads, key_heads, preferred_element_type=jnp.float32
    ) * HDIM ** (-0.5)
    probs_full = jnp.exp(scores_again - log_total[..., None])
    grad_probs = jnp.einsum(
        "ishd,ithd->ihst", grad_context, value_heads, preferred_element_type=jnp.float32
    )
    grad_scores = (
        probs_full
        * (grad_probs - jnp.sum(probs_full * grad_probs, axis=-1, keepdims=True))
        * HDIM ** (-0.5)
    ).astype(jnp.bfloat16)
    probs_bf = probs_full.astype(jnp.bfloat16)
    grad_value = jnp.einsum(
        "ihst,ishd->ithd", probs_bf, grad_context, preferred_element_type=jnp.float32
    ).reshape(-1, D)
    grad_query = jnp.einsum(
        "ihst,ithd->ishd", grad_scores, key_heads, preferred_element_type=jnp.float32
    ).reshape(-1, D)
    grad_key = jnp.einsum(
        "ihst,ishd->ithd", grad_scores, query_heads, preferred_element_type=jnp.float32
    ).reshape(-1, D)
    grad_mixed = jnp.concatenate([grad_query, grad_key, grad_value], axis=1).astype(jnp.bfloat16)
    proj_term = jnp.dot(act_one.T, grad_mixed, preferred_element_type=jnp.float32)
    grad_act = jnp.dot(grad_mixed, back_proj.T, preferred_element_type=jnp.float32)
    grad_tok_norm, gain_one_term, shift_one_term = norm_back(
        grad_act, normed_one, inv_one, back_gain_one.astype(jnp.float32)
    )
    tokens_grad = (grad_resid + grad_tok_norm).astype(jnp.bfloat16).reshape(tokens.shape)
    query_shift_term = jnp.sum(grad_query, axis=0)
    value_shift_term = jnp.sum(grad_value, axis=0)
    late = lax.psum_scatter(
        lane_pad(
            [
                proj_term.astype(jnp.bfloat16),
                jnp.stack(
                    [gain_one_term, shift_one_term, query_shift_term, value_shift_term], axis=0
                )
                .astype(jnp.bfloat16)
                .T,
            ]
        ),
        "shard",
        scatter_dimension=0,
        tiled=True,
    )
    early_sum = early.astype(jnp.float32)
    for other in other_replicas(early):
        early_sum = early_sum + other.astype(jnp.float32)
    late_sum = late.astype(jnp.float32)
    for other in other_replicas(late):
        late_sum = late_sum + other.astype(jnp.float32)
    late_small = late_sum[:, width_in:]
    early_small = early_sum[:, D:]
    dense_grads = (
        late_small[:, 0],
        late_small[:, 1],
        late_sum[:, :width_in],
        late_small[:, 2],
        late_small[:, 3],
        early_sum[:, :D],
        early_small[:, 0],
        early_small[:, 1],
        early_small[:, 2],
        early_small[:, 3 : 3 + experts],
    )
    return (
        block_out,
        tokens_grad,
        dense_grads[0],
        dense_grads[1],
        dense_grads[2],
        dense_grads[3],
        dense_grads[4],
        dense_grads[5],
        dense_grads[6],
        dense_grads[7],
        dense_grads[8],
        dense_grads[9],
        expert_grads[0],
        expert_grads[1],
        expert_grads[2],
        expert_grads[3],
    )


def solution(mesh):
    in_specs = (
        P(("replica", "shard"), None, None),
        P(("replica", "shard"), None, None),
        P("shard"),
        P("shard"),
        P("shard", None),
        P("shard"),
        P("shard"),
        P("shard", None),
        P("shard"),
        P("shard"),
        P("shard"),
        P("shard", None),
        P("shard", None, None),
        P("shard", None),
        P("shard", None, None),
        P("shard", None),
        P(("replica", "shard"), None),
        P(("replica", "shard"), None),
    )
    out_specs = (
        P(("replica", "shard"), None, None),
        P(("replica", "shard"), None, None),
        P("shard"),
        P("shard"),
        P("shard", None),
        P("shard"),
        P("shard"),
        P("shard", None),
        P("shard"),
        P("shard"),
        P("shard"),
        P("shard", None),
        P("shard", None, "replica"),
        P("shard", "replica"),
        P("shard", "replica", None),
        P("shard", "replica"),
    )
    return jax.shard_map(body, mesh=mesh, in_specs=in_specs, out_specs=out_specs, check_vma=False)
```

time: 635 us -> 344 us (0.54)
  blocking collectives: 177 us -> 0 us
  waiting for transfers between devices: 281 us -> 196 us
  other arithmetic: 34.6 us -> 12.7 us
    unnamed x2 -> x0, blocking collectives: 125 us -> none
    reduce_scatter x4 -> x1, waiting for transfers between devices: 169 us -> 46.2 us  [body(): lax.psum_scatter(lane_pad([proj_term.astype(jnp.bfloat16), jnp.stack([gai...]
    unnamed x13 -> x5, waiting for transfers between devices: 74.2 us -> 0.75 us
    all_gather x2, waiting for transfers between devices: 6.65 us -> 74.6 us  [the longest x1 46.3 us: body(): lax.all_gather(lane_pad([proj_in, small, router]), 'shard', axis=0, tiled...]
    ppermute x0 -> x3, waiting for transfers between devices: none -> 28.2 us  [other_replicas(): lax.ppermute(value, 'replica', [(at, (at + step) % size) for at in range(...]
    all_gather x1 -> x0, blocking collectives: 26.3 us -> none  [body(): lax.all_gather(router, 'shard', axis=0, tiled=True)]
    all_to_all x1 -> x0, blocking collectives: 20.7 us -> none  [body(): lax.all_to_all(grad_buffer, 'shard', split_axis=0, concat_axis=1, tiled=T...]
    unnamed x122 -> x48, local copies, waits for them, and re-layouts: 22.3 us -> 4.82 us
  transfers between devices with their start and end apart: 13 -> 9, of which waited for: 10 -> 7; matrix products, arithmetic and copies ran while one was open for 13% -> 22% of each run, Pallas kernels for 0% -> 0%
where the time goes in v1:
time: 344 us; the launch traced here: 343 us
  waiting for transfers between devices  196 us (57%)
  matrix products  76.7 us (22%)
  local copies, waits for them, and re-layouts  26.3 us (8%)
  starting transfers between devices  16.8 us (5%)
  between operations  14.4 us (4%)
  other arithmetic  12.7 us (4%)
    all_gather x1, waiting for transfers between devices, body(): lax.all_gather(lane_pad([proj_in, small, router]), 'shard', axis=0, tiled...  46.3 us
    reduce_scatter x1, waiting for transfers between devices, body(): lax.psum_scatter(lane_pad([proj_term.astype(jnp.bfloat16), jnp.stack([gai...  46.2 us
    all_gather x1, waiting for transfers between devices, body(): outproj_full = lax.all_gather(proj_out, 'shard', axis=0, tiled=True)  28.4 us
    ppermute x3, waiting for transfers between devices, other_replicas(): lax.ppermute(value, 'replica', [(at, (at + step) % size) for at in range(...  28.2 us
    all_to_all x1, waiting for transfers between devices, body(): lax.all_to_all(outgoing, 'shard', split_axis=0, concat_axis=0, tiled=True)  25 us
    all_to_all x1, waiting for transfers between devices, body(): lax.all_to_all(answer, 'shard', split_axis=0, concat_axis=0, tiled=True)  21 us
    dot_general x2, matrix products, expert_middle(): jnp.einsum('ecd,efd->ecf', grad_rows, down_weight, preferred_element_type...  8.57 us
    concatenate x3, local copies, waits for them, and re-layouts, lane_pad(): jnp.concatenate(blocks + [jnp.zeros((rows, spare), blocks[0].dtype)], axi...  8.55 us
  transfers between devices with their start and end apart: 9, of which 7 were waited for; matrix products, arithmetic and copies ran while one was open for 22% of the time, Pallas kernels for 0%

profile of v1, /device:TPU:0, one launch (start us, length us, event | category | flops | bytes accessed | tf_op | source)
XLA Modules:
  0.0 342.7 jit_solution(2914189716971794444)
XLA Ops:
  19.7 46.3 %all-gather.3.cloned.1.call-done = bf16[768,2432]{1,0:T(8,128)(2,1)} async-done(((bf16[48,2432]{1,0:T(8,128)(2,1)}), bf16[768,2432]{1,0:T(8,128)(2,1)}) %all-gather.3.cloned.1.call-update) | async-done | bytes 3735568 | tf_op jit(solution)/shard_map/all_gather | solution.py:128
  67.8 3.0 fusion.23
  73.4 3.5 %convolution_convert_fusion.4 = bf16[12,64,197]{2,1,0:T(8,128)(2,1)S(1)} fusion(bf16[197,12,64]{0,2,1:T(8,128)(2,1)S(1)} %bitcast.198, f32[12,197,197]{1,2,0:T(8,128)} %fusion.160), kind=kOutput, calls=%fused_computation.74 | convolution fusion | flops 61627312 | bytes 2468016 | tf_op jit(solution)/shard_map/ihst,ithd->ishd/dot_general | solution.py:162
  77.0 28.4 %all-gather.5.cloned.1.call-done = bf16[768,768]{1,0:T(8,128)(2,1)} async-done(((bf16[48,768]{1,0:T(8,128)(2,1)}), bf16[768,768]{1,0:T(8,128)(2,1)}) %all-gather.5.cloned.1.call-update) | async-done | bytes 1179664 | tf_op jit(solution)/shard_map/all_gather | solution.py:131
  111.3 4.5 %all-to-all-start = ((bf16[16,24,1536]{2,1,0:T(8,128)(2,1)}), bf16[16,24,1536]{2,1,0:T(8,128)(2,1)}, u32[]{:S(2)}, u32[]{:S(2)}) async-start(bf16[16,24,1536]{2,1,0:T(8,128)(2,1)} %pad_maximum_fusion.3), calls=%async_computation | async-start | bytes 2359296 | tf_op jit(solution)/shard_map/all_to_all | solution.py:199
  115.9 25.0 %all-to-all-done = bf16[16,24,1536]{2,1,0:T(8,128)(2,1)} async-done(((bf16[16,24,1536]{2,1,0:T(8,128)(2,1)}), bf16[16,24,1536]{2,1,0:T(8,128)(2,1)}, u32[]{:S(2)}, u32[]{:S(2)}) %all-to-all-start) | async-done | bytes 1179680 | tf_op jit(solution)/shard_map/all_to_all | solution.py:199
  140.9 5.8 %multiply_convert_fusion = (bf16[384,3072]{1,0:T(8,128)(2,1)S(1)}, f32[384,3072]{1,0:T(8,128)S(1)}) fusion(f32[3072]{0:T(1024)S(1)} %bitcast.220, bf16[1,768,3072]{2,1,0:T(8,128)(2,1)} %param.30, bf16[1,384,1536]{2,1,0:T(8,128)(2,1)} %bitcast.23), kind=kOutput, calls=%fused_computation.19 | convolution fusion | flops 1819017216 | bytes 12398592 | tf_op jit(solution)/shard_map/ecd,edf->ecf/dot_general | solution.py:92
  146.7 4.9 %fusion.7 = bf16[384,3072]{1,0:T(8,128)(2,1)S(1)} fusion(f32[384,3072]{1,0:T(8,128)S(1)} %get-tuple-element.110, bf16[1,3072,768]{2,1,0:T(8,128)(2,1)S(1)} %bitcast.237, bf16[1,384,1536]{2,1,0:T(8,128)(2,1)} %bitcast.23), kind=kOutput, calls=%fused_computation.9 | convolution fusion | flops 1823735808 | bytes 12386304 | tf_op jit(solution)/shard_map/ecd,efd->ecf/dot_general | solution.py:96
  157.0 7.4 %all-to-all-start.1 = ((bf16[16,24,1536]{2,1,0:T(8,128)(2,1)}), bf16[16,24,1536]{2,1,0:T(8,128)(2,1)S(1)}, u32[]{:S(2)}, u32[]{:S(2)}) async-start(bf16[16,24,1536]{2,1,0:T(8,128)(2,1)} %pad_maximum_fusion.4), calls=%async_computation.1 | async-start | bytes 2359296 | tf_op jit(solution)/shard_map/all_to_all | solution.py:214
  164.7 3.7 %fusion.27 = f32[12,197,197]{1,2,0:T(8,128)} fusion(bf16[197,12,64]{0,2,1:T(8,128)(2,1)S(1)} %bitcast.196, bf16[197,12,64]{0,2,1:T(8,128)(2,1)} %bitcast.201), kind=kOutput, calls=%fused_computation.34 | convolution fusion | flops 120620928 | bytes 2468016 | tf_op jit(solution)/shard_map/reduce_sum | solution.py:159
  168.4 21.0 %all-to-all-done.1 = bf16[16,24,1536]{2,1,0:T(8,128)(2,1)S(1)} async-done(((bf16[16,24,1536]{2,1,0:T(8,128)(2,1)}), bf16[16,24,1536]{2,1,0:T(8,128)(2,1)S(1)}, u32[]{:S(2)}, u32[]{:S(2)}) %all-to-all-start.1) | async-done | bytes 1179680 | tf_op jit(solution)/shard_map/all_to_all | solution.py:214
  198.9 3.5 %fusion.153 = (bf16[12,64]{1,0:T(8,128)(2,1)S(1)}, bf16[1,197,12,64]{1,3,2,0:T(8,128)(2,1)S(1)}) fusion(bf16[197,12,64]{0,2,1:T(8,128)(2,1)S(1)} %bitcast.203, f32[12,197,197]{1,2,0:T(8,128)} %fusion.160), kind=kOutput, calls=%fused_computation.215 | convolution fusion | flops 61777840 | bytes 2469552 | tf_op jit(solution)/shard_map/ihst,ishd->ithd/dot_general | solution.py:312
  204.4 4.9 %fusion.152 = (bf16[12,64]{1,0:T(8,128)(2,1)S(1)}, bf16[1,197,12,64]{1,3,2,0:T(8,128)(2,1)S(1)}) fusion(bf16[197,12,64]{0,2,1:T(8,128)(2,1)S(1)} %bitcast.202, f32[12,197,197]{1,2,0:T(8,128)} %fusion.27, f32[12,197,197]{1,2,0:T(8,128)} %fusion.161), kind=kOutput, calls=%fused_computation.214 | convolution fusion | flops 62243548 | bytes 4332384 | tf_op jit(solution)/shard_map/ihst,ithd->ishd/dot_general | solution.py:315
  209.4 4.9 %fusion.65 = bf16[12,64,197]{2,1,0:T(8,128)(2,1)S(1)} fusion(bf16[197,12,64]{0,2,1:T(8,128)(2,1)S(1)} %bitcast.197, f32[12,197,197]{1,2,0:T(8,128)} %fusion.27, f32[12,197,197]{1,2,0:T(8,128)} %fusion.161), kind=kOutput, calls=%fused_computation.73 | convolution fusion | flops 62093020 | bytes 4330848 | tf_op jit(solution)/shard_map/ihst,ishd->ithd/dot_general | solution.py:318
  214.3 4.3 %fusion.90 = (bf16[768]{0:T(1024)(128)(2,1)S(1)}, f32[197]{0:T(256)S(1)}, f32[197]{0:T(256)S(1)}, bf16[768]{0:T(1024)(128)(2,1)S(1)}, f32[197,768]{1,0:T(8,128)}) fusion(bf16[1,197,768]{2,1,0:T(8,128)(2,1)S(1)} %copy-done, f32[197]{0:T(256)S(1)} %add_rsqrt_fusion.1, f32[197]{0:T(256)S(1)} %broadcast_multiply_fusion.5, f32[768]{0:T(1024)S(1)} %get-tuple-element.84, ...), kind=kOutput, calls=%fused_computation.112 | convolution fusion | flops 701406336 | bytes 5363792 | tf_op jit(solution)/shard_map/dot_general | solution.py:323
  218.9 3.1 convolution_convert_fusion
  222.0 6.7 %concatenate.63 = bf16[768,2432]{1,0:T(8,128)(2,1)} concatenate(bf16[768,2304]{1,0:T(8,128)(2,1)} %convolution_convert_fusion, bf16[768,4]{1,0:T(8,128)(2,1)S(1)} %bitcast.207, bf16[768,124]{1,0:T(8,128)(2,1)S(1)} %broadcast_in_dim.12), dimensions={1} | concatenate | bytes 7471104 | tf_op jit(solution)/shard_map/concatenate | solution.py:61
  232.5 25.3 %collective-permute-done.2 = bf16[1,384,1536]{2,1,0:T(8,128)(2,1)S(1)} collective-permute-done((bf16[1,384,1536]{2,1,0:T(8,128)(2,1)}, bf16[1,384,1536]{2,1,0:T(8,128)(2,1)S(1)}, u32[]{:S(2)}, u32[]{:S(2)}) %collective-permute-start.2) | collective-permute-done | bytes 1179680 | tf_op jit(solution)/shard_map/ppermute | solution.py:67
  257.9 2.7 convolution_add_fusion
  260.6 3.7 %fusion.26 = bf16[1,384,1536]{2,1,0:T(8,128)(2,1)S(1)} fusion(f32[384,1536]{1,0:T(8,128)S(1)} %convolution_add_fusion, bf16[1,3072,768]{2,1,0:T(8,128)(2,1)} %param.32, s32[]{:T(128)S(6)} %select_n.21, bf16[1,384,1536]{2,1,0:T(8,128)(2,1)S(1)} %collective-permute-done.2), kind=kOutput, calls=%fused_computation.32 | convolution fusion | flops 911867904 | bytes 6488068 | tf_op jit(solution)/shard_map/ecd,efd->ecf/dot_general | solution.py:96
  267.7 5.4 %convolution_bitcast_fusion = f32[1,1536,768]{2,1,0:T(8,128)} fusion(bf16[1,384,1536]{2,1,0:T(8,128)(2,1)S(1)} %fusion.71, bf16[1,384,1536]{2,1,0:T(8,128)(2,1)S(1)} %dynamic-slice_bitcast_fusion, bf16[1,384,1536]{2,1,0:T(8,128)(2,1)S(1)} %collective-permute-done.2, bf16[1,384,1536]{2,1,0:T(8,128)(2,1)} %bitcast.23), kind=kOutput, calls=%fused_computation.22 | convolution fusion | flops 1819017216 | bytes 9437184 | tf_op jit(solution)/shard_map/ecf,ecd->efd/dot_general | solution.py:240
  273.0 5.4 %convolution_bitcast_fusion.1 = f32[1,768,1536]{2,1,0:T(8,128)} fusion(bf16[1,384,1536]{2,1,0:T(8,128)(2,1)S(1)} %fusion.26, bf16[1,384,1536]{2,1,0:T(8,128)(2,1)S(1)} %dynamic-slice_bitcast_fusion.1, bf16[1,384,1536]{2,1,0:T(8,128)(2,1)} %bitcast.23, bf16[1,384,1536]{2,1,0:T(8,128)(2,1)S(1)} %collective-permute-done.2), kind=kOutput, calls=%fused_computation.23 | convolution fusion | flops 1819017216 | bytes 9437184 | tf_op jit(solution)/shard_map/ecd,ecf->edf/dot_general | solution.py:238
  282.1 46.2 %reduce-scatter.5.cloned.1.call-done = bf16[48,2432]{1,0:T(8,128)(2,1)} async-done(((bf16[768,2432]{1,0:T(8,128)(2,1)}), bf16[48,2432]{1,0:T(8,128)(2,1)}) %reduce-scatter.5.cloned.1.call-update) | async-done | bytes 233488 | tf_op jit(solution)/shard_map/reduce_scatter | solution.py:330
  331.7 2.9 collective-permute-done
  (148 shorter events, 55.9 us)
Async XLA Ops:
  7.2 60.6 %copy-start = (bf16[1,197,768]{2,1,0:T(8,128)(2,1)S(1)}, bf16[1,197,768]{2,1,0:T(8,128)(2,1)}, u32[]{:S(2)}) copy-start(bf16[1,197,768]{2,1,0:T(8,128)(2,1)} %param.18) | copy-start | bytes 907780
  7.2 58.8 %all-gather.3.cloned.1.call-start = ((), (), s32[]{:S(2)}) async-start(), calls=%async_computation.4 | async-start | bytes 3969024 | tf_op jit(solution)/shard_map/all_gather | solution.py:128
  15.1 90.2 %all-gather.5.cloned.1.call-start = ((), (), s32[]{:S(2)}) async-start(), calls=%async_computation.5 | async-start | bytes 1253376 | tf_op jit(solution)/shard_map/all_gather | solution.py:131
  71.1 5.8 %copy-start.4 = (bf16[197,768]{0,1:T(8,128)(2,1)}, bf16[197,768]{0,1:T(8,128)(2,1)S(1)}, u32[]{:S(2)}) copy-start(bf16[197,768]{0,1:T(8,128)(2,1)S(1)} %copy.84) | copy-start | bytes 907780
  71.3 93.4 %copy-start.2 = (bf16[197,768]{0,1:T(8,128)(2,1)}, bf16[197,768]{0,1:T(8,128)(2,1)S(1)}, u32[]{:S(2)}) copy-start(bf16[197,768]{0,1:T(8,128)(2,1)S(1)} %copy.85) | copy-start | bytes 907780
  71.5 5.5 %copy-start.6 = (bf16[197,768]{0,1:T(8,128)(2,1)}, bf16[197,768]{0,1:T(8,128)(2,1)S(1)}, u32[]{:S(2)}) copy-start(bf16[197,768]{0,1:T(8,128)(2,1)S(1)} %copy.86) | copy-start | bytes 907780
  76.9 31.2 %copy-start.8 = (bf16[12,64,197]{2,1,0:T(8,128)(2,1)}, bf16[12,64,197]{2,1,0:T(8,128)(2,1)S(1)}, u32[]{:S(2)}) copy-start(bf16[12,64,197]{2,1,0:T(8,128)(2,1)S(1)} %convolution_convert_fusion.4) | copy-start | bytes 907780
  110.2 5.7 %copy-start.16 = (bf16[1,3072]{1,0:T(2,128)(2,1)S(1)}, bf16[1,3072]{1,0:T(2,128)(2,1)}, u32[]{:S(2)}) copy-start(bf16[1,3072]{1,0:T(2,128)(2,1)} %param.31) | copy-start | bytes 18436
  110.2 5.7 %copy-start.17 = (bf16[1,768]{1,0:T(2,128)(2,1)S(1)}, bf16[1,768]{1,0:T(2,128)(2,1)}, u32[]{:S(2)}) copy-start(bf16[1,768]{1,0:T(2,128)(2,1)} %param.33) | copy-start | bytes 4612
  111.3 35.4 %slice-start.2 = ((s8[4718592]{0:T(1024)(128)(4,1)}), s8[524288]{0:T(1024)(128)(4,1)S(1)}, s32[]{:S(2)}) async-start(s8[4718592]{0:T(1024)(128)(4,1)} %bitcast.236), calls=%async_computation.10 | async-start | bytes 1048576
  111.3 29.6 %all-to-all-start = ((bf16[16,24,1536]{2,1,0:T(8,128)(2,1)}), bf16[16,24,1536]{2,1,0:T(8,128)(2,1)}, u32[]{:S(2)}, u32[]{:S(2)}) async-start(bf16[16,24,1536]{2,1,0:T(8,128)(2,1)} %pad_maximum_fusion.3), calls=%async_computation | async-start | bytes 2359296 | tf_op jit(solution)/shard_map/all_to_all | solution.py:199
  140.9 5.8 %slice-start.3 = ((s8[4718592]{0:T(1024)(128)(4,1)}), s8[4194304]{0:T(1024)(128)(4,1)S(1)}, s32[]{:S(2)}) async-start(s8[4718592]{0:T(1024)(128)(4,1)} %bitcast.236), calls=%async_computation.11 | async-start | bytes 8388608
  140.9 10.7 %slice-start = ((s8[4718592]{0:T(1024)(128)(4,1)}), s8[4194304]{0:T(1024)(128)(4,1)S(1)}, s32[]{:S(2)}) async-start(s8[4718592]{0:T(1024)(128)(4,1)} %bitcast.234), calls=%async_computation.8 | async-start | bytes 8388608
  146.7 7.0 %copy-start.12 = (bf16[384,3072]{1,0:T(8,128)(2,1)}, bf16[384,3072]{1,0:T(8,128)(2,1)S(1)}, u32[]{:S(2)}) copy-start(bf16[384,3072]{1,0:T(8,128)(2,1)S(1)} %get-tuple-element.109) | copy-start | bytes 7077892
  146.7 4.9 %slice-start.1 = ((s8[4718592]{0:T(1024)(128)(4,1)}), s8[524288]{0:T(1024)(128)(4,1)S(1)}, s32[]{:S(2)}) async-start(s8[4718592]{0:T(1024)(128)(4,1)} %bitcast.234), calls=%async_computation.9 | async-start | bytes 1048576
  157.0 32.4 %all-to-all-start.1 = ((bf16[16,24,1536]{2,1,0:T(8,128)(2,1)}), bf16[16,24,1536]{2,1,0:T(8,128)(2,1)S(1)}, u32[]{:S(2)}, u32[]{:S(2)}) async-start(bf16[16,24,1536]{2,1,0:T(8,128)(2,1)} %pad_maximum_fusion.4), calls=%async_computation.1 | async-start | bytes 2359296 | tf_op jit(solution)/shard_map/all_to_all | solution.py:214
  164.4 114.1 %reduce-scatter.7.cloned.1.call-start = ((), (), s32[]{:S(2)}) async-start(), calls=%async_computation.7 | async-start | bytes 1462272
  196.8 131.5 %reduce-scatter.5.cloned.1.call-start = ((), (), s32[]{:S(2)}) async-start(), calls=%async_computation.6 | async-start | bytes 3969024 | tf_op jit(solution)/shard_map/reduce_scatter | solution.py:330
  204.4 5.0 %copy-start.3 = (bf16[197,768]{0,1:T(8,128)(2,1)S(1)}, bf16[197,768]{0,1:T(8,128)(2,1)}, u32[]{:S(2)}) copy-start(bf16[197,768]{0,1:T(8,128)(2,1)} %copy-done.2) | copy-start | bytes 907780
  228.8 29.1 %collective-permute-start.2 = (bf16[1,384,1536]{2,1,0:T(8,128)(2,1)}, bf16[1,384,1536]{2,1,0:T(8,128)(2,1)S(1)}, u32[]{:S(2)}, u32[]{:S(2)}) collective-permute-start(bf16[1,384,1536]{2,1,0:T(8,128)(2,1)} %bitcast.23), channel_id=1, source_target_pairs={{0,16},{16,0},{1,17},{17,1},{2,18},{18,2},{3,19},{19,3},{4,20},{20... | collective-permute-start | bytes 3538952 | tf_op jit(solution)/shard_map/ppermute | solution.py:67
  273.0 8.1 %copy-start.10 = (f32[197,768]{1,0:T(8,128)S(1)}, f32[197,768]{1,0:T(8,128)}, u32[]{:S(2)}) copy-start(f32[197,768]{1,0:T(8,128)} %get-tuple-element.114) | copy-start | bytes 1815556
  279.5 50.2 %collective-permute-start.1 = (bf16[48,896]{0,1:T(8,128)(2,1)S(1)}, bf16[48,896]{0,1:T(8,128)(2,1)S(1)}, u32[]{:S(2)}, u32[]{:S(2)}) collective-permute-start(bf16[48,896]{0,1:T(8,128)(2,1)S(1)} %copy.99), channel_id=1, source_target_pairs={{0,16},{16,0},{1,17},{17,1},{2,18},{18,2},{3,19},{19,3},{4,20},{20... | collective-permute-start | bytes 258056 | tf_op jit(solution)/shard_map/ppermute | solution.py:67
  328.3 6.3 %copy-start.15 = (bf16[48,2432]{1,0:T(8,128)(2,1)S(1)}, bf16[48,2432]{1,0:T(8,128)(2,1)}, u32[]{:S(2)}) copy-start(bf16[48,2432]{1,0:T(8,128)(2,1)} %reduce-scatter.5.cloned.1.call-done) | copy-start | bytes 700420
  328.3 6.3 %collective-permute-start = (bf16[48,2432]{1,0:T(8,128)(2,1)}, bf16[48,2432]{1,0:T(8,128)(2,1)S(1)}, u32[]{:S(2)}, u32[]{:S(2)}) collective-permute-start(bf16[48,2432]{1,0:T(8,128)(2,1)} %reduce-scatter.5.cloned.1.call-done), channel_id=1, source_target_pairs={{0,16},{16,0},{1,17},{17,1},{2,18},{18,2},{3,19},{19,3},{4,20},{20... | collective-permute-start | bytes 700424 | tf_op jit(solution)/shard_map/ppermute | solution.py:67
  (7 other events, 18.7 us)
Sparse Core Ops, SparseCore 0:
  15.2 50.7 all-gather.2
  68.3 36.9 all-gather.4
  196.9 60.0 reduce-scatter.6
  260.8 67.4 reduce-scatter.4

commit v2 on v1

--- a/solution.py
+++ b/solution.py
@@ -126,12 +126,13 @@
     )
     width_in, width_small = proj_in.shape[1], small.shape[1] + router.shape[1]
     first = lax.all_gather(
-        lane_pad([proj_in, small, router]), "shard", axis=0, tiled=True
-    )
-    outproj_full = lax.all_gather(proj_out, "shard", axis=0, tiled=True)
+        lane_pad([proj_in, proj_out, small, router]), "shard", axis=0, tiled=True
+    )
+    width_both = width_in + proj_out.shape[1]
     proj_full = first[:, :width_in]
-    small_full = first[:, width_in : width_in + small.shape[1]]
-    router_full = first[:, width_in + small.shape[1] : width_in + width_small]
+    outproj_full = first[:, width_in:width_both]
+    small_full = first[:, width_both : width_both + small.shape[1]]
+    router_full = first[:, width_both + small.shape[1] : width_both + width_small]
     (
         gain_one,
         shift_one,
@@ -277,20 +278,6 @@
     resid_bf = grad_resid.astype(jnp.bfloat16)
     out_shift_term = jnp.sum(grad_resid, axis=0)
     outproj_term = jnp.dot(context.T, resid_bf, preferred_element_type=jnp.float32)
-    early = lax.psum_scatter(
-        lane_pad(
-            [
-                outproj_term.astype(jnp.bfloat16),
-                jnp.stack([out_shift_term, gain_two_term, shift_two_term], axis=0)
-                .astype(jnp.bfloat16)
-                .T,
-                router_term.astype(jnp.bfloat16),
-            ]
-        ),
-        "shard",
-        scatter_dimension=0,
-        tiled=True,
-    )
     grad_context = (
         jnp.dot(resid_bf, back_outproj.T, preferred_element_type=jnp.float32)
         .astype(jnp.bfloat16)
@@ -327,40 +314,44 @@
     tokens_grad = (grad_resid + grad_tok_norm).astype(jnp.bfloat16).reshape(tokens.shape)
     query_shift_term = jnp.sum(grad_query, axis=0)
     value_shift_term = jnp.sum(grad_value, axis=0)
-    late = lax.psum_scatter(
+    column_sums = [
+        gain_one_term,
+        shift_one_term,
+        query_shift_term,
+        value_shift_term,
+        out_shift_term,
+        gain_two_term,
+        shift_two_term,
+    ]
+    summed = lax.psum_scatter(
         lane_pad(
             [
                 proj_term.astype(jnp.bfloat16),
-                jnp.stack(
-                    [gain_one_term, shift_one_term, query_shift_term, value_shift_term], axis=0
-                )
-                .astype(jnp.bfloat16)
-                .T,
+                outproj_term.astype(jnp.bfloat16),
+                jnp.stack(column_sums, axis=0).astype(jnp.bfloat16).T,
+                router_term.astype(jnp.bfloat16),
             ]
         ),
         "shard",
         scatter_dimension=0,
         tiled=True,
     )
-    early_sum = early.astype(jnp.float32)
-    for other in other_replicas(early):
-        early_sum = early_sum + other.astype(jnp.float32)
-    late_sum = late.astype(jnp.float32)
-    for other in other_replicas(late):
-        late_sum = late_sum + other.astype(jnp.float32)
-    late_small = late_sum[:, width_in:]
-    early_small = early_sum[:, D:]
+    total = summed.astype(jnp.float32)
+    for other in other_replicas(summed):
+        total = total + other.astype(jnp.float32)
+    small_total = total[:, width_both:]
+    columns = len(column_sums)
     dense_grads = (
-        late_small[:, 0],
-        late_small[:, 1],
-        late_sum[:, :width_in],
-        late_small[:, 2],
-        late_small[:, 3],
-        early_sum[:, :D],
-        early_small[:, 0],
-        early_small[:, 1],
-        early_small[:, 2],
-        early_small[:, 3 : 3 + experts],
+        small_total[:, 0],
+        small_total[:, 1],
+        total[:, :width_in],
+        small_total[:, 2],
+        small_total[:, 3],
+        total[:, width_in:width_both],
+        small_total[:, 4],
+        small_total[:, 5],
+        small_total[:, 6],
+        small_total[:, columns : columns + experts],
     )
     return (
         block_out,

time: 344 us -> 304 us (0.88)
  waiting for transfers between devices: 196 us -> 158 us
    all_gather x2 -> x1, waiting for transfers between devices: 74.6 us -> 51.9 us  [body(): lax.all_gather(lane_pad([proj_in, proj_out, small, router]), 'shard', axi...]
    reduce_scatter x1, waiting for transfers between devices: 46.2 us -> 31.3 us  [body(): lax.psum_scatter(lane_pad([proj_term.astype(jnp.bfloat16), outproj_term.a...]
    concatenate x3 -> x2, local copies, waits for them, and re-layouts: 8.55 us -> 10.2 us  [lane_pad(): jnp.concatenate(blocks + [jnp.zeros((rows, spare), blocks[0].dtype)], axi...]
    ppermute x3 -> x2, waiting for transfers between devices: 28.2 us -> 29.2 us  [other_replicas(): lax.ppermute(value, 'replica', [(at, (at + step) % size) for at in range(...]
  transfers between devices with their start and end apart: 9 -> 6, of which waited for: 7 -> 6; matrix products, arithmetic and copies ran while one was open for 22% -> 10% of each run, Pallas kernels for 0% -> 0%
where the time goes in v2:
time: 304 us; the launch traced here: 303 us
  waiting for transfers between devices  158 us (52%)
  matrix products  73.5 us (24%)
  local copies, waits for them, and re-layouts  28.2 us (9%)
  between operations  14.8 us (5%)
  starting transfers between devices  14.5 us (5%)
  other arithmetic  14.2 us (5%)
    all_gather x1, waiting for transfers between devices, body(): lax.all_gather(lane_pad([proj_in, proj_out, small, router]), 'shard', axi...  51.9 us
    reduce_scatter x1, waiting for transfers between devices, body(): lax.psum_scatter(lane_pad([proj_term.astype(jnp.bfloat16), outproj_term.a...  31.3 us
    ppermute x2, waiting for transfers between devices, other_replicas(): lax.ppermute(value, 'replica', [(at, (at + step) % size) for at in range(...  29.2 us
    all_to_all x1, waiting for transfers between devices, body(): lax.all_to_all(outgoing, 'shard', split_axis=0, concat_axis=0, tiled=True)  24.8 us
    all_to_all x1, waiting for transfers between devices, body(): lax.all_to_all(answer, 'shard', split_axis=0, concat_axis=0, tiled=True)  21 us
    concatenate x2, local copies, waits for them, and re-layouts, lane_pad(): jnp.concatenate(blocks + [jnp.zeros((rows, spare), blocks[0].dtype)], axi...  10.2 us
    dot_general x2, matrix products, expert_middle(): jnp.einsum('ecd,efd->ecf', grad_rows, down_weight, preferred_element_type...  9.2 us
    dot_general x2, matrix products, expert_middle(): jnp.einsum('ecd,edf->ecf', rows, up_weight, preferred_element_type=jnp.fl...  9 us
  transfers between devices with their start and end apart: 6, of which 6 were waited for; matrix products, arithmetic and copies ran while one was open for 10% of the time, Pallas kernels for 0%

profile of v2, /device:TPU:0, one launch (start us, length us, event | category | flops | bytes accessed | tf_op | source)
XLA Modules:
  0.0 303.3 jit_solution(2568404631235837072)
XLA Ops:
  20.3 51.9 %all-gather.2.cloned.1.call-done = bf16[768,3200]{1,0:T(8,128)(2,1)} async-done(((bf16[48,3200]{1,0:T(8,128)(2,1)}), bf16[768,3200]{1,0:T(8,128)(2,1)}) %all-gather.2.cloned.1.call-update) | async-done | bytes 4915216 | tf_op jit(solution)/shard_map/all_gather | solution.py:128
  74.4 3.0 fusion.23
  88.4 3.9 %all-to-all-start = ((bf16[16,24,1536]{2,1,0:T(8,128)(2,1)}), bf16[16,24,1536]{2,1,0:T(8,128)(2,1)S(1)}, u32[]{:S(2)}, u32[]{:S(2)}) async-start(bf16[16,24,1536]{2,1,0:T(8,128)(2,1)} %pad_maximum_fusion.3), calls=%async_computation | async-start | bytes 2359296 | tf_op jit(solution)/shard_map/all_to_all | solution.py:200
  92.4 24.8 %all-to-all-done = bf16[16,24,1536]{2,1,0:T(8,128)(2,1)S(1)} async-done(((bf16[16,24,1536]{2,1,0:T(8,128)(2,1)}), bf16[16,24,1536]{2,1,0:T(8,128)(2,1)S(1)}, u32[]{:S(2)}, u32[]{:S(2)}) %all-to-all-start) | async-done | bytes 1179680 | tf_op jit(solution)/shard_map/all_to_all | solution.py:200
  117.2 6.0 %multiply_convert_fusion = (bf16[384,3072]{1,0:T(8,128)(2,1)S(1)}, f32[384,3072]{1,0:T(8,128)S(1)}) fusion(f32[3072]{0:T(1024)S(1)} %bitcast.215, bf16[1,768,3072]{2,1,0:T(8,128)(2,1)} %param.30, bf16[1,384,1536]{2,1,0:T(8,128)(2,1)S(1)} %bitcast.182), kind=kOutput, calls=%fused_computation.19 | convolution fusion | flops 1819017216 | bytes 12398592 | tf_op jit(solution)/shard_map/ecd,edf->ecf/dot_general | solution.py:92
  123.2 5.5 %fusion.7 = bf16[384,3072]{1,0:T(8,128)(2,1)S(1)} fusion(f32[384,3072]{1,0:T(8,128)S(1)} %get-tuple-element.126, bf16[1,3072,768]{2,1,0:T(8,128)(2,1)} %param.32, bf16[1,384,1536]{2,1,0:T(8,128)(2,1)S(1)} %bitcast.183), kind=kOutput, calls=%fused_computation.9 | convolution fusion | flops 1823735808 | bytes 12386304 | tf_op jit(solution)/shard_map/ecd,efd->ecf/dot_general | solution.py:96
  128.8 2.0 fusion.58
  134.1 7.4 %all-to-all-start.1 = ((bf16[16,24,1536]{2,1,0:T(8,128)(2,1)}), bf16[16,24,1536]{2,1,0:T(8,128)(2,1)S(1)}, u32[]{:S(2)}, u32[]{:S(2)}) async-start(bf16[16,24,1536]{2,1,0:T(8,128)(2,1)} %pad_maximum_fusion.4), calls=%async_computation.1 | async-start | bytes 2359296 | tf_op jit(solution)/shard_map/all_to_all | solution.py:215
  141.7 3.7 %fusion.27 = f32[12,197,197]{1,2,0:T(8,128)} fusion(bf16[197,12,64]{0,2,1:T(8,128)(2,1)} %bitcast.196, bf16[197,12,64]{0,2,1:T(8,128)(2,1)S(1)} %bitcast.191), kind=kOutput, calls=%fused_computation.34 | convolution fusion | flops 120620928 | bytes 2468016 | tf_op jit(solution)/shard_map/reduce_sum | solution.py:160
  145.4 21.0 %all-to-all-done.1 = bf16[16,24,1536]{2,1,0:T(8,128)(2,1)S(1)} async-done(((bf16[16,24,1536]{2,1,0:T(8,128)(2,1)}), bf16[16,24,1536]{2,1,0:T(8,128)(2,1)S(1)}, u32[]{:S(2)}, u32[]{:S(2)}) %all-to-all-start.1) | async-done | bytes 1179680 | tf_op jit(solution)/shard_map/all_to_all | solution.py:215
  172.3 3.5 %fusion.154 = (bf16[12,64]{1,0:T(8,128)(2,1)S(1)}, bf16[1,197,12,64]{1,3,2,0:T(8,128)(2,1)S(1)}) fusion(bf16[197,12,64]{0,2,1:T(8,128)(2,1)S(1)} %bitcast.198, f32[12,197,197]{1,2,0:T(8,128)} %copy-done.4), kind=kOutput, calls=%fused_computation.212 | convolution fusion | flops 61777840 | bytes 2469552 | tf_op jit(solution)/shard_map/ihst,ishd->ithd/dot_general | solution.py:299
  177.8 5.4 %fusion.65 = bf16[12,64,197]{2,1,0:T(8,128)(2,1)} fusion(bf16[197,12,64]{0,2,1:T(8,128)(2,1)S(1)} %bitcast.197, f32[12,197,197]{1,2,0:T(8,128)} %fusion.27, f32[12,197,197]{1,2,0:T(8,128)} %fusion.163), kind=kOutput, calls=%fused_computation.72 | convolution fusion | flops 62093020 | bytes 4330848 | tf_op jit(solution)/shard_map/ihst,ishd->ithd/dot_general | solution.py:305
  183.2 5.4 %fusion.155 = (bf16[12,64]{1,0:T(8,128)(2,1)S(1)}, bf16[1,197,12,64]{1,3,2,0:T(8,128)(2,1)}) fusion(bf16[197,12,64]{0,2,1:T(8,128)(2,1)S(1)} %bitcast.192, f32[12,197,197]{1,2,0:T(8,128)} %fusion.27, f32[12,197,197]{1,2,0:T(8,128)} %fusion.163), kind=kOutput, calls=%fused_computation.213 | convolution fusion | flops 62243548 | bytes 4332384 | tf_op jit(solution)/shard_map/ihst,ithd->ishd/dot_general | solution.py:302
  189.7 3.1 %convolution_convert_fusion = bf16[768,2304]{1,0:T(8,128)(2,1)} fusion(bf16[197,768]{0,1:T(8,128)(2,1)S(1)} %bitcast.233, bf16[197,768]{0,1:T(8,128)(2,1)S(1)} %bitcast.235, bf16[197,768]{0,1:T(8,128)(2,1)S(1)} %bitcast.237, bf16[1,197,768]{2,1,0:T(8,128)(2,1)S(1)} %copy-done.2, f32[768]{0:T(1024)S(1)} %copy-done.34, f32[768]{0:T(1024)S(1)} %copy-done.21, ...), kind=kOutput, calls=%fused_computation.3 | convolution fusion | flops 702572544 | bytes 4757032 | tf_op jit(solution)/shard_map/dot_general | solution.py:309
  192.8 4.2 %fusion.92 = (bf16[768]{0:T(1024)(128)(2,1)S(1)}, f32[197]{0:T(256)S(1)}, f32[197]{0:T(256)S(1)}, bf16[768]{0:T(1024)(128)(2,1)S(1)}, f32[197,768]{1,0:T(8,128)}) fusion(bf16[1,197,768]{2,1,0:T(8,128)(2,1)S(1)} %copy-done.2, f32[197]{0:T(256)S(1)} %copy-done.32, f32[197]{0:T(256)S(1)} %copy-done.24, f32[768]{0:T(1024)S(1)} %copy-done.21, ...), kind=kOutput, calls=%fused_computation.113 | convolution fusion | flops 701406336 | bytes 5363792 | tf_op jit(solution)/shard_map/dot_general | solution.py:310
  197.7 8.4 %concatenate.60 = bf16[768,3200]{1,0:T(8,128)(2,1)} concatenate(bf16[768,2304]{1,0:T(8,128)(2,1)} %convolution_convert_fusion, bf16[768,768]{1,0:T(8,128)(2,1)S(1)} %convolution_convert_fusion.1, bf16[768,7]{1,0:T(8,128)(2,1)S(1)} %bitcast.200, bf16[768,16]{1,0:T(8,128)(2,1)S(1)} %copy.121, bf16[768,105]{1,0:T(8,128)(2,1)S(1)} %broadcast_in_dim.10), dimensions={1} | concatenate | bytes 9830400 | tf_op jit(solution)/shard_map/concatenate | solution.py:61
  211.0 25.2 %collective-permute-done.1 = bf16[1,384,1536]{2,1,0:T(8,128)(2,1)S(1)} collective-permute-done((bf16[1,384,1536]{2,1,0:T(8,128)(2,1)S(1)}, bf16[1,384,1536]{2,1,0:T(8,128)(2,1)S(1)}, u32[]{:S(2)}, u32[]{:S(2)}) %collective-permute-start.1) | collective-permute-done | bytes 1179680 | tf_op jit(solution)/shard_map/ppermute | solution.py:67
  236.2 3.0 convolution_add_fusion
  239.2 3.7 %fusion.26 = bf16[1,384,1536]{2,1,0:T(8,128)(2,1)S(1)} fusion(f32[384,1536]{1,0:T(8,128)S(1)} %convolution_add_fusion, bf16[1,3072,768]{2,1,0:T(8,128)(2,1)} %param.32, s32[]{:T(128)S(6)} %select_n.21, bf16[1,384,1536]{2,1,0:T(8,128)(2,1)S(1)} %collective-permute-done.1), kind=kOutput, calls=%fused_computation.32 | convolution fusion | flops 911867904 | bytes 6488068 | tf_op jit(solution)/shard_map/ecd,efd->ecf/dot_general | solution.py:96
  245.2 4.3 %convolution_bitcast_fusion = f32[1,1536,768]{2,1,0:T(8,128)} fusion(bf16[1,384,1536]{2,1,0:T(8,128)(2,1)S(1)} %fusion.71, bf16[1,384,1536]{2,1,0:T(8,128)(2,1)S(1)} %dynamic-slice_bitcast_fusion, bf16[1,384,1536]{2,1,0:T(8,128)(2,1)S(1)} %collective-permute-done.1, bf16[1,384,1536]{2,1,0:T(8,128)(2,1)S(1)} %bitcast.186), kind=kOutput, calls=%fused_computation.22 | convolution fusion | flops 1819017216 | bytes 9437184 | tf_op jit(solution)/shard_map/ecf,ecd->efd/dot_general | solution.py:241
  249.4 4.2 %convolution_bitcast_fusion.1 = f32[1,768,1536]{2,1,0:T(8,128)} fusion(bf16[1,384,1536]{2,1,0:T(8,128)(2,1)S(1)} %fusion.26, bf16[1,384,1536]{2,1,0:T(8,128)(2,1)S(1)} %dynamic-slice_bitcast_fusion.1, bf16[1,384,1536]{2,1,0:T(8,128)(2,1)S(1)} %bitcast.187, bf16[1,384,1536]{2,1,0:T(8,128)(2,1)S(1)} %collective-permute-done.1), kind=kOutput, calls=%fused_computation.23 | convolution fusion | flops 1819017216 | bytes 9437184 | tf_op jit(solution)/shard_map/ecd,ecf->edf/dot_general | solution.py:239
  253.7 31.3 %reduce-scatter.2.cloned.1.call-done = bf16[48,3200]{1,0:T(8,128)(2,1)} async-done(((bf16[768,3200]{1,0:T(8,128)(2,1)}), bf16[48,3200]{1,0:T(8,128)(2,1)}) %reduce-scatter.2.cloned.1.call-update) | async-done | bytes 307216 | tf_op jit(solution)/shard_map/reduce_scatter | solution.py:326
  286.4 2.1 fusion.118
  288.4 4.0 %collective-permute-done = bf16[48,3200]{1,0:T(8,128)(2,1)S(1)} collective-permute-done((bf16[48,3200]{1,0:T(8,128)(2,1)}, bf16[48,3200]{1,0:T(8,128)(2,1)S(1)}, u32[]{:S(2)}, u32[]{:S(2)}) %collective-permute-start) | collective-permute-done | bytes 307232 | tf_op jit(solution)/shard_map/ppermute | solution.py:67
  (173 shorter events, 51.6 us)
Async XLA Ops:
  7.2 67.2 %copy-start.2 = (bf16[1,197,768]{2,1,0:T(8,128)(2,1)S(1)}, bf16[1,197,768]{2,1,0:T(8,128)(2,1)}, u32[]{:S(2)}) copy-start(bf16[1,197,768]{2,1,0:T(8,128)(2,1)} %param.18) | copy-start | bytes 907780
  7.2 65.0 %all-gather.2.cloned.1.call-start = ((), (), s32[]{:S(2)}) async-start(), calls=%async_computation.3 | async-start | bytes 5222400 | tf_op jit(solution)/shard_map/all_gather | solution.py:128
  16.3 61.1 %copy-start.23 = (f32[197]{0:T(256)}, f32[197]{0:T(256)S(1)}, u32[]{:S(2)}) copy-start(f32[197]{0:T(256)S(1)} %broadcast_multiply_fusion.5) | copy-start | bytes 2368
  17.5 59.9 %copy-start.31 = (f32[197]{0:T(256)}, f32[197]{0:T(256)S(1)}, u32[]{:S(2)}) copy-start(f32[197]{0:T(256)S(1)} %add_rsqrt_fusion.1) | copy-start | bytes 2368
  88.4 28.7 %all-to-all-start = ((bf16[16,24,1536]{2,1,0:T(8,128)(2,1)}), bf16[16,24,1536]{2,1,0:T(8,128)(2,1)S(1)}, u32[]{:S(2)}, u32[]{:S(2)}) async-start(bf16[16,24,1536]{2,1,0:T(8,128)(2,1)} %pad_maximum_fusion.3), calls=%async_computation | async-start | bytes 2359296 | tf_op jit(solution)/shard_map/all_to_all | solution.py:200
  117.1 6.1 %copy-start = (bf16[16,24,1536]{2,1,0:T(8,128)(2,1)}, bf16[16,24,1536]{2,1,0:T(8,128)(2,1)S(1)}, u32[]{:S(2)}) copy-start(bf16[16,24,1536]{2,1,0:T(8,128)(2,1)S(1)} %all-to-all-done) | copy-start | bytes 3538948
  117.1 11.6 %slice-start = ((s8[4718592]{0:T(1024)(128)(4,1)}), s8[4194304]{0:T(1024)(128)(4,1)S(1)}, s32[]{:S(2)}) async-start(s8[4718592]{0:T(1024)(128)(4,1)} %bitcast.229), calls=%async_computation.5 | async-start | bytes 8388608
  117.1 13.8 %slice-start.2 = ((s8[4718592]{0:T(1024)(128)(4,1)}), s8[4194304]{0:T(1024)(128)(4,1)S(1)}, s32[]{:S(2)}) async-start(s8[4718592]{0:T(1024)(128)(4,1)} %bitcast.231), calls=%async_computation.7 | async-start | bytes 8388608
  123.2 7.7 %copy-start.13 = (bf16[384,3072]{1,0:T(8,128)(2,1)}, bf16[384,3072]{1,0:T(8,128)(2,1)S(1)}, u32[]{:S(2)}) copy-start(bf16[384,3072]{1,0:T(8,128)(2,1)S(1)} %get-tuple-element.125) | copy-start | bytes 7077892
  123.2 5.6 %slice-start.1 = ((s8[4718592]{0:T(1024)(128)(4,1)}), s8[524288]{0:T(1024)(128)(4,1)S(1)}, s32[]{:S(2)}) async-start(s8[4718592]{0:T(1024)(128)(4,1)} %bitcast.229), calls=%async_computation.6 | async-start | bytes 1048576
  123.2 7.7 %slice-start.3 = ((s8[4718592]{0:T(1024)(128)(4,1)}), s8[524288]{0:T(1024)(128)(4,1)S(1)}, s32[]{:S(2)}) async-start(s8[4718592]{0:T(1024)(128)(4,1)} %bitcast.231), calls=%async_computation.8 | async-start | bytes 1048576
  132.9 8.8 %copy-start.6 = (bf16[197,768]{0,1:T(8,128)(2,1)S(1)}, bf16[197,768]{0,1:T(8,128)(2,1)}, u32[]{:S(2)}) copy-start(bf16[197,768]{0,1:T(8,128)(2,1)} %copy-done.5) | copy-start | bytes 907780
  134.1 32.4 %all-to-all-start.1 = ((bf16[16,24,1536]{2,1,0:T(8,128)(2,1)}), bf16[16,24,1536]{2,1,0:T(8,128)(2,1)S(1)}, u32[]{:S(2)}, u32[]{:S(2)}) async-start(bf16[16,24,1536]{2,1,0:T(8,128)(2,1)} %pad_maximum_fusion.4), calls=%async_computation.1 | async-start | bytes 2359296 | tf_op jit(solution)/shard_map/all_to_all | solution.py:215
  141.4 25.5 %copy-start.27 = (s32[197,1]{0,1:T(1,128)S(1)}, s32[197,1]{0,1:T(1,128)}, u32[]{:S(2)}) copy-start(s32[197,1]{0,1:T(1,128)} %copy-done.25) | copy-start | bytes 2368
  141.4 25.5 %copy-start.30 = (s32[197,1]{0,1:T(1,128)S(1)}, s32[197,1]{0,1:T(1,128)}, u32[]{:S(2)}) copy-start(s32[197,1]{0,1:T(1,128)} %copy-done.28) | copy-start | bytes 2368
  141.5 143.5 %reduce-scatter.2.cloned.1.call-start = ((), (), s32[]{:S(2)}) async-start(), calls=%async_computation.4 | async-start | bytes 5222400 | tf_op jit(solution)/shard_map/reduce_scatter | solution.py:326
  175.8 7.4 %copy-start.7 = (bf16[197,768]{0,1:T(8,128)(2,1)S(1)}, bf16[197,768]{0,1:T(8,128)(2,1)}, u32[]{:S(2)}) copy-start(bf16[197,768]{0,1:T(8,128)(2,1)} %copy-done.5) | copy-start | bytes 907780
  183.2 5.4 %copy-start.16 = (bf16[12,64,197]{2,1,0:T(8,128)(2,1)S(1)}, bf16[12,64,197]{2,1,0:T(8,128)(2,1)}, u32[]{:S(2)}) copy-start(bf16[12,64,197]{2,1,0:T(8,128)(2,1)} %convolution_convert_fusion.4) | copy-start | bytes 907780
  183.2 6.1 %copy-start.21 = (f32[768]{0:T(1024)S(1)}, f32[768]{0:T(1024)}, u32[]{:S(2)}) copy-start(f32[768]{0:T(1024)} %copy-done.20) | copy-start | bytes 9220
  183.2 6.1 %copy-start.24 = (f32[197]{0:T(256)S(1)}, f32[197]{0:T(256)}, u32[]{:S(2)}) copy-start(f32[197]{0:T(256)} %copy-done.23) | copy-start | bytes 2368
  183.2 6.1 %copy-start.32 = (f32[197]{0:T(256)S(1)}, f32[197]{0:T(256)}, u32[]{:S(2)}) copy-start(f32[197]{0:T(256)} %copy-done.31) | copy-start | bytes 2368
  183.2 6.1 %copy-start.34 = (f32[768]{0:T(1024)S(1)}, f32[768]{0:T(1024)}, u32[]{:S(2)}) copy-start(f32[768]{0:T(1024)} %copy-done.33) | copy-start | bytes 9220
  207.4 28.8 %collective-permute-start.1 = (bf16[1,384,1536]{2,1,0:T(8,128)(2,1)S(1)}, bf16[1,384,1536]{2,1,0:T(8,128)(2,1)S(1)}, u32[]{:S(2)}, u32[]{:S(2)}) collective-permute-start(bf16[1,384,1536]{2,1,0:T(8,128)(2,1)S(1)} %bitcast.184), channel_id=1, source_target_pairs={{0,16},{16,0},{1,17},{17,1},{2,18},{18,2},{3,19},{19,3},{4,20},{20... | collective-permute-start | bytes 3538952 | tf_op jit(solution)/shard_map/ppermute | solution.py:67
  284.9 7.5 %collective-permute-start = (bf16[48,3200]{1,0:T(8,128)(2,1)}, bf16[48,3200]{1,0:T(8,128)(2,1)S(1)}, u32[]{:S(2)}, u32[]{:S(2)}) collective-permute-start(bf16[48,3200]{1,0:T(8,128)(2,1)} %reduce-scatter.2.cloned.1.call-done), channel_id=1, source_target_pairs={{0,16},{16,0},{1,17},{17,1},{2,18},{18,2},{3,19},{19,3},{4,20},{20... | collective-permute-start | bytes 921608 | tf_op jit(solution)/shard_map/ppermute | solution.py:67
  (24 other events, 65.2 us)
Sparse Core Ops, SparseCore 0:
  15.3 56.8 all-gather.1
  206.3 78.5 reduce-scatter.1

commit v3 on v2

--- a/solution.py
+++ b/solution.py
@@ -328,8 +328,14 @@
             [
                 proj_term.astype(jnp.bfloat16),
                 outproj_term.astype(jnp.bfloat16),
-                jnp.stack(column_sums, axis=0).astype(jnp.bfloat16).T,
-                router_term.astype(jnp.bfloat16),
+                lax.optimization_barrier(
+                    lane_pad(
+                        [
+                            jnp.stack(column_sums, axis=0).astype(jnp.bfloat16).T,
+                            router_term.astype(jnp.bfloat16),
+                        ]
+                    )
+                ),
             ]
         ),
         "shard",

time: 304 us -> 302 us (level)
  local copies, waits for them, and re-layouts: 28.2 us -> 19.9 us
  other arithmetic: 14.2 us -> 19.4 us
    concatenate x2, local copies, waits for them, and re-layouts: 10.2 us -> 2.41 us  [lane_pad(): jnp.concatenate(blocks + [jnp.zeros((rows, spare), blocks[0].dtype)], axi...]
    concatenate x0 -> x2, other arithmetic: none -> 5.25 us  [lane_pad(): jnp.concatenate(blocks + [jnp.zeros((rows, spare), blocks[0].dtype)], axi...]
where the time goes in v3:
time: 302 us; the launch traced here: 301 us
  waiting for transfers between devices  158 us (52%)
  matrix products  74.7 us (25%)
  local copies, waits for them, and re-layouts  19.9 us (7%)
  other arithmetic  19.4 us (6%)
  between operations  14.8 us (5%)
  starting transfers between devices  14.5 us (5%)
    all_gather x1, waiting for transfers between devices, body(): lax.all_gather(lane_pad([proj_in, proj_out, small, router]), 'shard', axi...  51.9 us
    reduce_scatter x1, waiting for transfers between devices, body(): lax.psum_scatter(lane_pad([proj_term.astype(jnp.bfloat16), outproj_term.a...  31.2 us
    ppermute x2, waiting for transfers between devices, other_replicas(): lax.ppermute(value, 'replica', [(at, (at + step) % size) for at in range(...  29.3 us
    all_to_all x1, waiting for transfers between devices, body(): lax.all_to_all(outgoing, 'shard', split_axis=0, concat_axis=0, tiled=True)  24.8 us
    all_to_all x1, waiting for transfers between devices, body(): lax.all_to_all(answer, 'shard', split_axis=0, concat_axis=0, tiled=True)  20.5 us
    dot_general x2, matrix products, expert_middle(): jnp.einsum('ecd,efd->ecf', grad_rows, down_weight, preferred_element_type...  9.2 us
    dot_general x2, matrix products, expert_middle(): jnp.einsum('ecd,edf->ecf', rows, up_weight, preferred_element_type=jnp.fl...  8.98 us
    all_to_all x1, starting transfers between devices, body(): lax.all_to_all(answer, 'shard', split_axis=0, concat_axis=0, tiled=True)  7.4 us
  transfers between devices with their start and end apart: 6, of which 6 were waited for; matrix products, arithmetic and copies ran while one was open for 10% of the time, Pallas kernels for 0%

profile of v3, /device:TPU:0, one launch (start us, length us, event | category | flops | bytes accessed | tf_op | source)
XLA Modules:
  0.0 300.9 jit_solution(4956869069759141743)
XLA Ops:
  20.3 51.9 %all-gather.2.cloned.1.call-done = bf16[768,3200]{1,0:T(8,128)(2,1)} async-done(((bf16[48,3200]{1,0:T(8,128)(2,1)}), bf16[768,3200]{1,0:T(8,128)(2,1)}) %all-gather.2.cloned.1.call-update) | async-done | bytes 4915216 | tf_op jit(solution)/shard_map/all_gather | solution.py:128
  74.4 3.0 fusion.23
  88.4 3.9 %all-to-all-start = ((bf16[16,24,1536]{2,1,0:T(8,128)(2,1)}), bf16[16,24,1536]{2,1,0:T(8,128)(2,1)S(1)}, u32[]{:S(2)}, u32[]{:S(2)}) async-start(bf16[16,24,1536]{2,1,0:T(8,128)(2,1)} %pad_maximum_fusion.4), calls=%async_computation | async-start | bytes 2359296 | tf_op jit(solution)/shard_map/all_to_all | solution.py:200
  92.4 24.8 %all-to-all-done = bf16[16,24,1536]{2,1,0:T(8,128)(2,1)S(1)} async-done(((bf16[16,24,1536]{2,1,0:T(8,128)(2,1)}), bf16[16,24,1536]{2,1,0:T(8,128)(2,1)S(1)}, u32[]{:S(2)}, u32[]{:S(2)}) %all-to-all-start) | async-done | bytes 1179680 | tf_op jit(solution)/shard_map/all_to_all | solution.py:200
  117.2 6.0 %multiply_convert_fusion = (bf16[384,3072]{1,0:T(8,128)(2,1)S(1)}, f32[384,3072]{1,0:T(8,128)S(1)}) fusion(f32[3072]{0:T(1024)S(1)} %bitcast.215, bf16[1,768,3072]{2,1,0:T(8,128)(2,1)} %param.30, bf16[1,384,1536]{2,1,0:T(8,128)(2,1)S(1)} %bitcast.182), kind=kOutput, calls=%fused_computation.20 | convolution fusion | flops 1819017216 | bytes 12398592 | tf_op jit(solution)/shard_map/ecd,edf->ecf/dot_general | solution.py:92
  123.2 5.5 %fusion.7 = bf16[384,3072]{1,0:T(8,128)(2,1)S(1)} fusion(f32[384,3072]{1,0:T(8,128)S(1)} %get-tuple-element.126, bf16[1,3072,768]{2,1,0:T(8,128)(2,1)} %param.32, bf16[1,384,1536]{2,1,0:T(8,128)(2,1)S(1)} %bitcast.183), kind=kOutput, calls=%fused_computation.10 | convolution fusion | flops 1823735808 | bytes 12386304 | tf_op jit(solution)/shard_map/ecd,efd->ecf/dot_general | solution.py:96
  128.8 2.0 fusion.58
  134.1 7.4 %all-to-all-start.1 = ((bf16[16,24,1536]{2,1,0:T(8,128)(2,1)}), bf16[16,24,1536]{2,1,0:T(8,128)(2,1)S(1)}, u32[]{:S(2)}, u32[]{:S(2)}) async-start(bf16[16,24,1536]{2,1,0:T(8,128)(2,1)} %pad_maximum_fusion.5), calls=%async_computation.1 | async-start | bytes 2359296 | tf_op jit(solution)/shard_map/all_to_all | solution.py:215
  142.3 3.7 %fusion.27 = f32[12,197,197]{1,2,0:T(8,128)} fusion(bf16[197,12,64]{0,2,1:T(8,128)(2,1)} %bitcast.196, bf16[197,12,64]{0,2,1:T(8,128)(2,1)S(1)} %bitcast.191), kind=kOutput, calls=%fused_computation.35 | convolution fusion | flops 120620928 | bytes 2468016 | tf_op jit(solution)/shard_map/reduce_sum | solution.py:160
  146.0 20.5 %all-to-all-done.1 = bf16[16,24,1536]{2,1,0:T(8,128)(2,1)S(1)} async-done(((bf16[16,24,1536]{2,1,0:T(8,128)(2,1)}), bf16[16,24,1536]{2,1,0:T(8,128)(2,1)S(1)}, u32[]{:S(2)}, u32[]{:S(2)}) %all-to-all-start.1) | async-done | bytes 1179680 | tf_op jit(solution)/shard_map/all_to_all | solution.py:215
  172.4 3.5 %fusion.154 = (bf16[12,64]{1,0:T(8,128)(2,1)S(1)}, bf16[1,197,12,64]{1,3,2,0:T(8,128)(2,1)S(1)}) fusion(bf16[197,12,64]{0,2,1:T(8,128)(2,1)S(1)} %bitcast.198, f32[12,197,197]{1,2,0:T(8,128)} %copy-done.4), kind=kOutput, calls=%fused_computation.214 | convolution fusion | flops 61777840 | bytes 2469552 | tf_op jit(solution)/shard_map/ihst,ishd->ithd/dot_general | solution.py:299
  177.8 5.4 %fusion.65 = bf16[12,64,197]{2,1,0:T(8,128)(2,1)} fusion(bf16[197,12,64]{0,2,1:T(8,128)(2,1)S(1)} %bitcast.197, f32[12,197,197]{1,2,0:T(8,128)} %fusion.27, f32[12,197,197]{1,2,0:T(8,128)} %fusion.163), kind=kOutput, calls=%fused_computation.73 | convolution fusion | flops 62093020 | bytes 4330848 | tf_op jit(solution)/shard_map/ihst,ishd->ithd/dot_general | solution.py:305
  183.2 5.4 %fusion.155 = (bf16[12,64]{1,0:T(8,128)(2,1)S(1)}, bf16[1,197,12,64]{1,3,2,0:T(8,128)(2,1)}) fusion(bf16[197,12,64]{0,2,1:T(8,128)(2,1)S(1)} %bitcast.192, f32[12,197,197]{1,2,0:T(8,128)} %fusion.27, f32[12,197,197]{1,2,0:T(8,128)} %fusion.163), kind=kOutput, calls=%fused_computation.215 | convolution fusion | flops 62243548 | bytes 4332384 | tf_op jit(solution)/shard_map/ihst,ithd->ishd/dot_general | solution.py:302
  189.5 4.3 %convolution_convert_fusion = bf16[768,2304]{1,0:T(8,128)(2,1)} fusion(bf16[197,768]{0,1:T(8,128)(2,1)S(1)} %bitcast.233, bf16[197,768]{0,1:T(8,128)(2,1)} %bitcast.235, bf16[197,768]{0,1:T(8,128)(2,1)} %bitcast.237, bf16[1,197,768]{2,1,0:T(8,128)(2,1)S(1)} %copy-done.2, f32[768]{0:T(1024)S(1)} %copy-done.34, f32[768]{0:T(1024)S(1)} %copy-done.21, ...), kind=kOutput, calls=%fused_computation.3 | convolution fusion | flops 702572544 | bytes 4757032 | tf_op jit(solution)/shard_map/dot_general | solution.py:309
  193.8 4.2 %fusion.92 = (bf16[768]{0:T(1024)(128)(2,1)S(1)}, f32[197]{0:T(256)S(1)}, f32[197]{0:T(256)S(1)}, bf16[768]{0:T(1024)(128)(2,1)S(1)}, f32[197,768]{1,0:T(8,128)}) fusion(bf16[1,197,768]{2,1,0:T(8,128)(2,1)S(1)} %copy-done.2, f32[197]{0:T(256)S(1)} %copy-done.32, f32[197]{0:T(256)S(1)} %copy-done.24, f32[768]{0:T(1024)S(1)} %copy-done.21, ...), kind=kOutput, calls=%fused_computation.114 | convolution fusion | flops 701406336 | bytes 5363792 | tf_op jit(solution)/shard_map/dot_general | solution.py:310
  198.7 5.1 %pad_maximum_fusion = bf16[768,3200]{1,0:T(8,128)(2,1)} fusion(bf16[768,128]{1,0:T(8,128)(2,1)S(1)} %maximum_maximum_fusion, bf16[768,768]{1,0:T(8,128)(2,1)S(1)} %convolution_convert_fusion.1, bf16[768,2304]{1,0:T(8,128)(2,1)} %convolution_convert_fusion), kind=kLoop, calls=%fused_computation.4 | loop fusion | flops 14745600 | bytes 9830400 | tf_op jit(solution)/shard_map/concatenate | solution.py:61
  208.6 25.2 %collective-permute-done.1 = bf16[1,384,1536]{2,1,0:T(8,128)(2,1)S(1)} collective-permute-done((bf16[1,384,1536]{2,1,0:T(8,128)(2,1)S(1)}, bf16[1,384,1536]{2,1,0:T(8,128)(2,1)S(1)}, u32[]{:S(2)}, u32[]{:S(2)}) %collective-permute-start.1) | collective-permute-done | bytes 1179680 | tf_op jit(solution)/shard_map/ppermute | solution.py:67
  233.8 2.9 convolution_add_fusion
  236.8 3.7 %fusion.26 = bf16[1,384,1536]{2,1,0:T(8,128)(2,1)S(1)} fusion(f32[384,1536]{1,0:T(8,128)S(1)} %convolution_add_fusion, bf16[1,3072,768]{2,1,0:T(8,128)(2,1)} %param.32, s32[]{:T(128)S(6)} %select_n.21, bf16[1,384,1536]{2,1,0:T(8,128)(2,1)S(1)} %collective-permute-done.1), kind=kOutput, calls=%fused_computation.33 | convolution fusion | flops 911867904 | bytes 6488068 | tf_op jit(solution)/shard_map/ecd,efd->ecf/dot_general | solution.py:96
  242.8 4.3 %convolution_bitcast_fusion = f32[1,1536,768]{2,1,0:T(8,128)} fusion(bf16[1,384,1536]{2,1,0:T(8,128)(2,1)S(1)} %fusion.71, bf16[1,384,1536]{2,1,0:T(8,128)(2,1)S(1)} %dynamic-slice_bitcast_fusion, bf16[1,384,1536]{2,1,0:T(8,128)(2,1)S(1)} %collective-permute-done.1, bf16[1,384,1536]{2,1,0:T(8,128)(2,1)S(1)} %bitcast.186), kind=kOutput, calls=%fused_computation.23 | convolution fusion | flops 1819017216 | bytes 9437184 | tf_op jit(solution)/shard_map/ecf,ecd->efd/dot_general | solution.py:241
  247.0 4.2 %convolution_bitcast_fusion.1 = f32[1,768,1536]{2,1,0:T(8,128)} fusion(bf16[1,384,1536]{2,1,0:T(8,128)(2,1)S(1)} %fusion.26, bf16[1,384,1536]{2,1,0:T(8,128)(2,1)S(1)} %dynamic-slice_bitcast_fusion.1, bf16[1,384,1536]{2,1,0:T(8,128)(2,1)S(1)} %bitcast.187, bf16[1,384,1536]{2,1,0:T(8,128)(2,1)S(1)} %collective-permute-done.1), kind=kOutput, calls=%fused_computation.24 | convolution fusion | flops 1819017216 | bytes 9437184 | tf_op jit(solution)/shard_map/ecd,ecf->edf/dot_general | solution.py:239
  251.3 31.2 %reduce-scatter.2.cloned.1.call-done = bf16[48,3200]{1,0:T(8,128)(2,1)} async-done(((bf16[768,3200]{1,0:T(8,128)(2,1)}), bf16[48,3200]{1,0:T(8,128)(2,1)}) %reduce-scatter.2.cloned.1.call-update) | async-done | bytes 307216 | tf_op jit(solution)/shard_map/reduce_scatter | solution.py:326
  283.9 2.1 fusion.118
  286.0 4.0 %collective-permute-done = bf16[48,3200]{1,0:T(8,128)(2,1)S(1)} collective-permute-done((bf16[48,3200]{1,0:T(8,128)(2,1)}, bf16[48,3200]{1,0:T(8,128)(2,1)S(1)}, u32[]{:S(2)}, u32[]{:S(2)}) %collective-permute-start) | collective-permute-done | bytes 307232 | tf_op jit(solution)/shard_map/ppermute | solution.py:67
  (177 shorter events, 51.9 us)
Async XLA Ops:
  7.2 67.2 %copy-start.2 = (bf16[1,197,768]{2,1,0:T(8,128)(2,1)S(1)}, bf16[1,197,768]{2,1,0:T(8,128)(2,1)}, u32[]{:S(2)}) copy-start(bf16[1,197,768]{2,1,0:T(8,128)(2,1)} %param.18) | copy-start | bytes 907780
  7.2 65.0 %all-gather.2.cloned.1.call-start = ((), (), s32[]{:S(2)}) async-start(), calls=%async_computation.3 | async-start | bytes 5222400 | tf_op jit(solution)/shard_map/all_gather | solution.py:128
  16.3 61.1 %copy-start.23 = (f32[197]{0:T(256)}, f32[197]{0:T(256)S(1)}, u32[]{:S(2)}) copy-start(f32[197]{0:T(256)S(1)} %broadcast_multiply_fusion.5) | copy-start | bytes 2368
  17.5 59.9 %copy-start.31 = (f32[197]{0:T(256)}, f32[197]{0:T(256)S(1)}, u32[]{:S(2)}) copy-start(f32[197]{0:T(256)S(1)} %add_rsqrt_fusion.1) | copy-start | bytes 2368
  88.4 28.7 %all-to-all-start = ((bf16[16,24,1536]{2,1,0:T(8,128)(2,1)}), bf16[16,24,1536]{2,1,0:T(8,128)(2,1)S(1)}, u32[]{:S(2)}, u32[]{:S(2)}) async-start(bf16[16,24,1536]{2,1,0:T(8,128)(2,1)} %pad_maximum_fusion.4), calls=%async_computation | async-start | bytes 2359296 | tf_op jit(solution)/shard_map/all_to_all | solution.py:200
  117.2 6.1 %copy-start = (bf16[16,24,1536]{2,1,0:T(8,128)(2,1)}, bf16[16,24,1536]{2,1,0:T(8,128)(2,1)S(1)}, u32[]{:S(2)}) copy-start(bf16[16,24,1536]{2,1,0:T(8,128)(2,1)S(1)} %all-to-all-done) | copy-start | bytes 3538948
  117.2 11.6 %slice-start = ((s8[4718592]{0:T(1024)(128)(4,1)}), s8[4194304]{0:T(1024)(128)(4,1)S(1)}, s32[]{:S(2)}) async-start(s8[4718592]{0:T(1024)(128)(4,1)} %bitcast.229), calls=%async_computation.5 | async-start | bytes 8388608
  117.2 13.7 %slice-start.2 = ((s8[4718592]{0:T(1024)(128)(4,1)}), s8[4194304]{0:T(1024)(128)(4,1)S(1)}, s32[]{:S(2)}) async-start(s8[4718592]{0:T(1024)(128)(4,1)} %bitcast.231), calls=%async_computation.7 | async-start | bytes 8388608
  123.2 7.7 %copy-start.13 = (bf16[384,3072]{1,0:T(8,128)(2,1)}, bf16[384,3072]{1,0:T(8,128)(2,1)S(1)}, u32[]{:S(2)}) copy-start(bf16[384,3072]{1,0:T(8,128)(2,1)S(1)} %get-tuple-element.125) | copy-start | bytes 7077892
  123.2 5.6 %slice-start.1 = ((s8[4718592]{0:T(1024)(128)(4,1)}), s8[524288]{0:T(1024)(128)(4,1)S(1)}, s32[]{:S(2)}) async-start(s8[4718592]{0:T(1024)(128)(4,1)} %bitcast.229), calls=%async_computation.6 | async-start | bytes 1048576
  123.2 7.7 %slice-start.3 = ((s8[4718592]{0:T(1024)(128)(4,1)}), s8[524288]{0:T(1024)(128)(4,1)S(1)}, s32[]{:S(2)}) async-start(s8[4718592]{0:T(1024)(128)(4,1)} %bitcast.231), calls=%async_computation.8 | async-start | bytes 1048576
  132.9 9.4 %copy-start.6 = (bf16[197,768]{0,1:T(8,128)(2,1)S(1)}, bf16[197,768]{0,1:T(8,128)(2,1)}, u32[]{:S(2)}) copy-start(bf16[197,768]{0,1:T(8,128)(2,1)} %copy-done.5) | copy-start | bytes 907780
  134.1 32.4 %all-to-all-start.1 = ((bf16[16,24,1536]{2,1,0:T(8,128)(2,1)}), bf16[16,24,1536]{2,1,0:T(8,128)(2,1)S(1)}, u32[]{:S(2)}, u32[]{:S(2)}) async-start(bf16[16,24,1536]{2,1,0:T(8,128)(2,1)} %pad_maximum_fusion.5), calls=%async_computation.1 | async-start | bytes 2359296 | tf_op jit(solution)/shard_map/all_to_all | solution.py:215
  141.5 141.0 %reduce-scatter.2.cloned.1.call-start = ((), (), s32[]{:S(2)}) async-start(), calls=%async_computation.4 | async-start | bytes 5222400 | tf_op jit(solution)/shard_map/reduce_scatter | solution.py:326
  142.3 24.7 %copy-start.27 = (s32[197,1]{0,1:T(1,128)S(1)}, s32[197,1]{0,1:T(1,128)}, u32[]{:S(2)}) copy-start(s32[197,1]{0,1:T(1,128)} %copy-done.25) | copy-start | bytes 2368
  142.3 24.7 %copy-start.30 = (s32[197,1]{0,1:T(1,128)S(1)}, s32[197,1]{0,1:T(1,128)}, u32[]{:S(2)}) copy-start(s32[197,1]{0,1:T(1,128)} %copy-done.28) | copy-start | bytes 2368
  175.8 7.4 %copy-start.7 = (bf16[197,768]{0,1:T(8,128)(2,1)S(1)}, bf16[197,768]{0,1:T(8,128)(2,1)}, u32[]{:S(2)}) copy-start(bf16[197,768]{0,1:T(8,128)(2,1)} %copy-done.5) | copy-start | bytes 907780
  183.2 5.6 %copy-start.16 = (bf16[12,64,197]{2,1,0:T(8,128)(2,1)S(1)}, bf16[12,64,197]{2,1,0:T(8,128)(2,1)}, u32[]{:S(2)}) copy-start(bf16[12,64,197]{2,1,0:T(8,128)(2,1)} %convolution_convert_fusion.4) | copy-start | bytes 907780
  183.2 6.3 %copy-start.21 = (f32[768]{0:T(1024)S(1)}, f32[768]{0:T(1024)}, u32[]{:S(2)}) copy-start(f32[768]{0:T(1024)} %copy-done.20) | copy-start | bytes 9220
  183.2 6.3 %copy-start.24 = (f32[197]{0:T(256)S(1)}, f32[197]{0:T(256)}, u32[]{:S(2)}) copy-start(f32[197]{0:T(256)} %copy-done.23) | copy-start | bytes 2368
  183.2 6.3 %copy-start.32 = (f32[197]{0:T(256)S(1)}, f32[197]{0:T(256)}, u32[]{:S(2)}) copy-start(f32[197]{0:T(256)} %copy-done.31) | copy-start | bytes 2368
  183.2 6.3 %copy-start.34 = (f32[768]{0:T(1024)S(1)}, f32[768]{0:T(1024)}, u32[]{:S(2)}) copy-start(f32[768]{0:T(1024)} %copy-done.33) | copy-start | bytes 9220
  205.0 28.8 %collective-permute-start.1 = (bf16[1,384,1536]{2,1,0:T(8,128)(2,1)S(1)}, bf16[1,384,1536]{2,1,0:T(8,128)(2,1)S(1)}, u32[]{:S(2)}, u32[]{:S(2)}) collective-permute-start(bf16[1,384,1536]{2,1,0:T(8,128)(2,1)S(1)} %bitcast.184), channel_id=1, source_target_pairs={{0,16},{16,0},{1,17},{17,1},{2,18},{18,2},{3,19},{19,3},{4,20},{20... | collective-permute-start | bytes 3538952 | tf_op jit(solution)/shard_map/ppermute | solution.py:67
  282.5 7.5 %collective-permute-start = (bf16[48,3200]{1,0:T(8,128)(2,1)}, bf16[48,3200]{1,0:T(8,128)(2,1)S(1)}, u32[]{:S(2)}, u32[]{:S(2)}) collective-permute-start(bf16[48,3200]{1,0:T(8,128)(2,1)} %reduce-scatter.2.cloned.1.call-done), channel_id=1, source_target_pairs={{0,16},{16,0},{1,17},{17,1},{2,18},{18,2},{3,19},{19,3},{4,20},{20... | collective-permute-start | bytes 921608 | tf_op jit(solution)/shard_map/ppermute | solution.py:67
  (25 other events, 76.5 us)
Sparse Core Ops, SparseCore 0:
  15.3 56.8 all-gather.1
  203.9 78.5 reduce-scatter.1
